TPU v7x, 32 devices: a whole 2x2x4 slice. The times are simulated.
32 devices in a mesh: img: 4 (over x, core), seq: 2 (over y), tp: 4 (over z).
Axes of the slice: x: 2, y: 2, z: 4, core: 2. Of those that a mesh axis runs over, the one named last changes fastest.
Arguments:
- vit_qkv: bfloat16 [4, 512, 3, 1280], P('img', ('seq', 'tp')), may hold values from -6 to 6
- patch_counts: int32 [4], P('img'), may hold values from 128 to 512, as said below
- vit_out_weight: bfloat16 [1280, 1280], replicated, may hold values from -0.15625 to 0.15625
- vit_norm_gain: float32 [1280], replicated, may hold values from 0.25 to 1.75
- merger_weight: bfloat16 [5120, 8192], P(('img', 'seq'), 'tp'), may hold values from -8 to 8
- lm_norm_gain: float32 [8192], P('tp'), may hold values from 0.25 to 1.75
- kv_weight: bfloat16 [8192, 2048], P('tp', ('img', 'seq')), may hold values from -0.0625 to 0.0625
- queries: bfloat16 [4, 1024, 64, 128], P('img', 'seq', 'tp'), may hold values from -6 to 6
- span_kv: bfloat16 [4, 1024, 2, 8, 128], P('img', 'seq', None, 'tp'), may hold values from -6 to 6
Outputs:
- lm_attention: bfloat16 [4, 1024, 64, 128], P('img', 'seq', 'tp')
Inputs may be any that keep to these rules, and one draw needn't show every extreme that they name: `patch_counts`: each count is a multiple of 4, at least 128, and some image has exactly 512.
All inputs are finite; a program needn't handle non-finite values.
Results may differ from a plain program's by a relative error of at most 0.04.
Values may be sent and summed in bfloat16 or wider, within the bound.
No kernel may reach another device: no remote copies, remote signals or barrier semaphores. Data moves between devices by JAX's collectives and lax.ppermute only.
A program may use at most 128 MiB of HBM per device.

v0:
```python
import jax
import jax.numpy as jnp
from jax import lax
from jax.sharding import PartitionSpec as P

VIT_D = 1280
VIT_HEADS = 16
VIT_HDIM = 80
D = 8192
HQ = 64
KVH = 8
HD = 128


masked_score = -1e30


def fold_block(running, scores, usable, value_block, forms):
    peak, weight_sum, blended = running
    scores = jnp.where(usable, scores, masked_score)
    new_peak = jnp.maximum(peak, jnp.max(scores, axis=-1))
    weights = jnp.where(usable, jnp.exp(scores - new_peak[..., None]), 0.0)
    decay = jnp.exp(peak - new_peak)
    weight_sum = weight_sum * decay + jnp.sum(weights, axis=-1)
    blended = blended * decay[..., None] + jnp.einsum(
        forms, weights.astype(jnp.bfloat16), value_block, preferred_element_type=jnp.float32
    )
    return (new_peak, weight_sum, blended)


def local(
    vit_qkv,
    patch_counts,
    vit_out_weight,
    vit_norm_gain,
    merger_weight,
    lm_norm_gain,
    kv_weight,
    queries,
    span_kv,
):
    patch_rows = vit_qkv.shape[1]
    tp_count = lax.axis_size("tp")
    seq_index = lax.axis_index("seq")
    tp_index = lax.axis_index("tp")
    patch_total = patch_counts[0]
    local_qkv = vit_qkv[0].reshape(patch_rows, 3, VIT_HEADS, VIT_HDIM)
    scaling = VIT_HDIM ** (-0.5)
    spread = lax.all_to_all(local_qkv, "seq", split_axis=2, concat_axis=0, tiled=True)
    local_rows = spread.shape[0]

    def seq_rows(index):
        source = index // local_rows
        within = index % local_rows
        return (within // patch_rows * tp_count + source) * patch_rows + within % patch_rows

    heads_local = spread.shape[2]
    query_count = spread.shape[0]
    query_rows = spread[:, 0]
    running = (
        jnp.full((heads_local, query_count), masked_score, jnp.float32),
        jnp.zeros((heads_local, query_count), jnp.float32),
        jnp.zeros((heads_local, query_count, VIT_HDIM), jnp.float32),
    )
    make_heads_local = query_rows.shape[1]
    key_piece = lax.all_gather(spread[:, 1], "tp", axis=0, tiled=True)
    value_piece = lax.all_gather(spread[:, 2], "tp", axis=0, tiled=True)
    blocks = key_piece.shape[0] // local_rows
    key_blocks = key_piece.reshape(blocks, local_rows, make_heads_local, VIT_HDIM)
    value_blocks = value_piece.reshape(blocks, local_rows, make_heads_local, VIT_HDIM)
    offsets = jnp.arange(blocks, dtype=jnp.int32) * local_rows

    def make_advance(state, inputs):
        key_block, value_block, offset = inputs
        usable = seq_rows(offset + jnp.arange(local_rows, dtype=jnp.int32)) < patch_total
        scores = (
            jnp.einsum("qhd,khd->hqk", query_rows, key_block, preferred_element_type=jnp.float32)
            * scaling
        )
        return (fold_block(state, scores, usable[None, None, :], value_block, "hqk,khd->hqd"), None)

    result, _ = lax.scan(make_advance, running, (key_blocks, value_blocks, offsets))
    state = result
    peak, weight_sum, blended = state
    returned = lax.all_to_all(
        jnp.transpose(blended / weight_sum[..., None], (1, 0, 2)).astype(jnp.bfloat16),
        "seq",
        split_axis=0,
        concat_axis=1,
        tiled=True,
    )
    attended = returned.reshape(patch_rows, VIT_D)
    hidden = jnp.dot(attended, vit_out_weight, preferred_element_type=jnp.float32)
    patch_ids = (seq_index * tp_count + tp_index) * patch_rows + jnp.arange(
        patch_rows, dtype=jnp.int32
    )
    hidden = jnp.where((patch_ids < patch_total)[:, None], hidden, 0.0)
    centred = hidden - jnp.mean(hidden, axis=-1, keepdims=True)
    spread_sq = jnp.mean(centred * centred, axis=-1, keepdims=True)
    normed = (centred * lax.rsqrt(spread_sq + 1e-06) * vit_norm_gain).astype(jnp.bfloat16)
    merged_local = normed.reshape(patch_rows // 4, 4 * VIT_D)
    token_rows = lax.all_gather(merged_local, "tp", axis=0, tiled=True)
    embedded_sum = jnp.dot(
        token_rows,
        lax.all_gather(merger_weight, ("img", "seq"), axis=0, tiled=True),
        preferred_element_type=jnp.float32,
    )
    embedded = lax.optimization_barrier(embedded_sum.astype(jnp.bfloat16))
    embedded_wide = embedded.astype(jnp.float32)
    square_sums = lax.psum(jnp.sum(embedded_wide * embedded_wide, axis=-1), "tp")
    lm_normed = (embedded_wide * lax.rsqrt(square_sums[:, None] / D + 1e-06) * lm_norm_gain).astype(
        jnp.bfloat16
    )
    kv_terms = jnp.dot(
        lm_normed,
        lax.all_gather(kv_weight, ("img", "seq"), axis=1, tiled=True),
        preferred_element_type=jnp.float32,
    )
    visual_count = kv_terms.shape[0]
    kv_terms = kv_terms.reshape(visual_count, 2, KVH, HD)
    visual_kv = lax.psum_scatter(
        kv_terms.astype(jnp.bfloat16), "tp", scatter_dimension=2, tiled=True
    )
    span_rows = queries.shape[1]
    kv_local = span_kv.shape[3]
    groups = HQ // KVH
    lm_scaling = HD ** (-0.5)
    grouped = queries[0].reshape(span_rows, kv_local, groups, HD)
    causal = jnp.arange(span_rows)[:, None] >= jnp.arange(span_rows)[None, :]
    near_scores = (
        jnp.einsum("ckgd,nkd->kgcn", grouped, span_kv[0, :, 0], preferred_element_type=jnp.float32)
        * lm_scaling
    )
    initial = (
        jnp.full((kv_local, groups, span_rows), masked_score, jnp.float32),
        jnp.zeros((kv_local, groups, span_rows), jnp.float32),
        jnp.zeros((kv_local, groups, span_rows, HD), jnp.float32),
    )
    initial = fold_block(
        initial, near_scores, causal[None, None], span_kv[0, :, 1], "kgcn,nkd->kgcd"
    )
    visual_total = patch_total // 4
    key_piece = lax.all_gather(visual_kv[:, 0], "seq", axis=0, tiled=True)
    value_piece = lax.all_gather(visual_kv[:, 1], "seq", axis=0, tiled=True)
    blocks = key_piece.shape[0] // visual_count
    key_blocks = key_piece.reshape(blocks, visual_count, kv_local, HD)
    value_blocks = value_piece.reshape(blocks, visual_count, kv_local, HD)
    offsets = jnp.arange(blocks, dtype=jnp.int32) * visual_count

    def visual_advance(state, inputs):
        key_block, value_block, offset = inputs
        usable = offset + jnp.arange(visual_count, dtype=jnp.int32) < visual_total
        scores = (
            jnp.einsum("ckgd,nkd->kgcn", grouped, key_block, preferred_element_type=jnp.float32)
            * lm_scaling
        )
        return (
            fold_block(state, scores, usable[None, None, None, :], value_block, "kgcn,nkd->kgcd"),
            None,
        )

    result, _ = lax.scan(visual_advance, initial, (key_blocks, value_blocks, offsets))
    peak, weight_sum, blended = result
    result = jnp.transpose(blended / weight_sum[..., None], (2, 0, 1, 3))
    return result.reshape(span_rows, kv_local * groups, HD).astype(jnp.bfloat16)[None]


def solution(mesh):
    placed = (
        P("img", ("seq", "tp"), None, None),
        P("img"),
        P(),
        P(),
        P(("img", "seq"), "tp"),
        P("tp"),
        P("tp", ("img", "seq")),
        P("img", "seq", "tp", None),
        P("img", "seq", None, "tp", None),
    )
    return jax.shard_map(
        local, mesh=mesh, in_specs=placed, out_specs=P("img", "seq", "tp", None), check_vma=False
    )
```

profile of v0, /device:TPU:0, one launch (start us, length us, event | category | flops | bytes accessed | tf_op | source)
XLA Modules:
  0.0 268.3 jit_solution(11138296800675128971)
XLA Ops:
  8.0 2.8 %reshape_squeeze.7 = bf16[64,3,16,80]{3,2,0,1:T(8,128)(2,1)} reshape(bf16[1,64,3,1280]{3,1,2,0:T(8,128)(2,1)} %param.13) | data formatting | bytes 983040 | tf_op jit(solution)/shard_map/reshape;squeeze | solution.py:47
  13.1 4.3 %all-to-all-start = ((bf16[64,3,16,80]{3,0,1,2:T(8,128)(2,1)}), bf16[64,3,16,80]{3,0,1,2:T(8,128)(2,1)}, u32[]{:S(2)}, u32[]{:S(2)}) async-start(bf16[64,3,16,80]{3,0,1,2:T(8,128)(2,1)} %copy.59), calls=%async_computation | async-start | bytes 1572864 | tf_op jit(solution)/shard_map/all_to_all | solution.py:49
  21.5 2.9 %fusion.39 = (f32[2,8,512]{2,1,0:T(8,128)S(1)}, f32[2,512,512,8]{2,1,3,0:T(8,128)S(1)}) fusion(pred[512,512]{0,1:T(8,128)(4,1)S(1)} %iota_compare_fusion, bf16[512,2,8,128]{3,0,2,1:T(8,128)(2,1)S(1)} %bitcast.153, bf16[1,512,1,2,128]{4,3,2,1,0:T(2,128)(2,1)S(1)} %get-tuple-element.345), kind=kOutput, calls=%fused_computation.63 | convolution fusion | flops 1086316544 | bytes 19431424 | tf_op jit(solution)/shard_map/ckgd,nkd->kgcn/dot_general | solution.py:131
  24.5 4.0 %fusion.41 = f32[2,8,512]{2,1,0:T(8,128)S(1)} fusion(f32[2,512,512,8]{2,1,3,0:T(8,128)S(1)} %get-tuple-element.351, f32[2,8,512]{2,1,0:T(8,128)S(1)} %broadcast_maximum_fusion, pred[512,512]{0,1:T(8,128)(4,1)S(1)} %iota_compare_fusion), kind=kLoop, calls=%fused_computation.65 | loop fusion | flops 20963328 | bytes 17104896 | tf_op jit(solution)/shard_map/reduce_sum | solution.py:24
  31.5 4.0 %all-to-all-done = bf16[64,3,16,80]{3,0,1,2:T(8,128)(2,1)} async-done(((bf16[64,3,16,80]{3,0,1,2:T(8,128)(2,1)}), bf16[64,3,16,80]{3,0,1,2:T(8,128)(2,1)}, u32[]{:S(2)}, u32[]{:S(2)}) %all-to-all-start) | async-done | bytes 491552 | tf_op jit(solution)/shard_map/all_to_all | solution.py:49
  39.2 17.9 %all-gather = bf16[512,1,8,80]{0,3,2,1:T(8,128)(2,1)} all-gather(bf16[128,1,8,80]{0,3,2,1:T(8,128)(2,1)S(1)} %copy.62), channel_id=2, replica_groups=mesh['img'=4,'seq'=2,'tp'=4] {'tp'}, dimensions={0}, use_global_device_ids=true | all-gather | bytes 819200 | tf_op jit(solution)/shard_map/all_gather | solution.py:66
  62.6 16.4 %all-gather.1 = bf16[512,1,8,80]{0,3,2,1:T(8,128)(2,1)} all-gather(bf16[128,1,8,80]{0,3,2,1:T(8,128)(2,1)S(1)} %copy.63), channel_id=3, replica_groups=mesh['img'=4,'seq'=2,'tp'=4] {'tp'}, dimensions={0}, use_global_device_ids=true | all-gather | bytes 819200 | tf_op jit(solution)/shard_map/all_gather | solution.py:67
  84.5 32.3 %while.33 = (s32[]{:T(128)}, f32[8,128]{1,0:T(8,128)S(1)}, f32[8,128]{1,0:T(8,128)S(1)}, f32[8,128,80]{1,2,0:T(8,128)}, s32[4]{0:T(128)}, /*index=5*/s32[]{:T(12...) while((s32[]{:T(128)}, f32[8,128]{1,0:T(8,128)S(1)}, ...), condition=%wide.region_5.6_spmd.clone, body=%wide.region_2.5_spmd.clone.sunk | while | flops 43379200 | bytes 2786957 | solution.py:82
  120.8 4.1 %all-to-all-start.1 = ((bf16[128,8,80]{2,1,0:T(8,128)(2,1)}), bf16[128,8,80]{2,1,0:T(8,128)(2,1)}, u32[]{:S(2)}, u32[]{:S(2)}) async-start(bf16[128,8,80]{2,1,0:T(8,128)(2,1)} %fusion.56), calls=%async_computation.1 | async-start | bytes 524288 | tf_op jit(solution)/shard_map/all_to_all | solution.py:85
  125.0 5.2 %all-to-all-done.1 = bf16[128,8,80]{2,1,0:T(8,128)(2,1)} async-done(((bf16[128,8,80]{2,1,0:T(8,128)(2,1)}), bf16[128,8,80]{2,1,0:T(8,128)(2,1)}, u32[]{:S(2)}, u32[]{:S(2)}) %all-to-all-start.1) | async-done | bytes 163872 | tf_op jit(solution)/shard_map/all_to_all | solution.py:85
  134.4 15.5 %all_gather.23 = bf16[64,5120]{1,0:T(8,128)(2,1)S(1)} all-gather(bf16[16,5120]{1,0:T(8,128)(2,1)S(1)} %reshape.140), channel_id=1, replica_groups=mesh['img'=4,'seq'=2,'tp'=4] {'tp'}, dimensions={0}, use_global_device_ids=true | all-gather | bytes 819200 | tf_op jit(solution)/shard_map/all_gather | solution.py:102
  149.9 9.7 %convolution_convert_fusion.1 = bf16[64,2048]{1,0:T(8,128)(2,1)S(1)} fusion(bf16[64,5120]{1,0:T(8,128)(2,1)S(1)} %all_gather.23, bf16[5120,2048]{1,0:T(8,128)(2,1)} %all-gather.7.cloned.1.call-done), kind=kOutput, calls=%fused_computation.71 | convolution fusion | flops 1342308352 | bytes 21889024 | tf_op jit(solution)/shard_map/dot_general | solution.py:103
  159.7 8.5 %psum.7 = f32[64]{0:T(128)S(1)} all-reduce(f32[64]{0:T(128)S(1)} %fusion.49), channel_id=1, replica_groups=mesh['img'=4,'seq'=2,'tp'=4] {'tp'}, use_global_device_ids=true, to_apply=%region_9.10 | all-reduce | flops 64 | bytes 512 | tf_op jit(solution)/shard_map/psum | solution.py:110
  168.2 15.8 %all-gather.9.cloned.1.call-done = bf16[2048,2048]{1,0:T(8,128)(2,1)} async-done(((bf16[2048,256]{1,0:T(8,128)(2,1)}), bf16[2048,2048]{1,0:T(8,128)(2,1)}) %all-gather.9.cloned.1.call-update) | async-done | bytes 8388624 | tf_op jit(solution)/shard_map/all_gather | solution.py:116
  184.1 5.0 %fusion.48 = bf16[8,8,16,128]{3,1,2,0:T(8,128)(2,1)S(1)} fusion(bf16[2048,2048]{1,0:T(8,128)(2,1)} %all-gather.9.cloned.1.call-done, bf16[64,2048]{1,0:T(8,128)(2,1)S(1)} %convolution_convert_fusion.1, f32[2048]{0:T(1024)S(1)} %copy-done.10, f32[64]{0:T(128)S(1)} %add_rsqrt_fusion), kind=kOutput, calls=%fused_computation.75 | convolution fusion | flops 537526272 | bytes 8921344 | tf_op jit(solution)/shard_map/dot_general | solution.py:114
  189.9 10.4 %broadcast_add_fusion = f32[2,8,512,128]{3,2,1,0:T(8,128)} fusion(f32[2,8,512]{2,1,0:T(8,128)S(1)} %get-tuple-element.348, f32[2,512,512,8]{2,1,3,0:T(8,128)} %copy-done.5, f32[2,8,512]{2,1,0:T(8,128)S(1)} %broadcast_maximum_fusion, pred[512,512]{0,1:T(8,128)(4,1)S(1)} %copy-done.7, bf16[1,512,1,2,128]{4,3,2,1,0:T(2,128)(2,1)S(1)} %copy-done.9), kind=kOutput, calls=%fused_computation.73 | convolution fusion | flops 1095761920 | bytes 21561344 | tf_op jit(solution)/shard_map/kgcn,nkd->kgcd/dot_general | solution.py:25
  201.7 24.0 %all-reduce.3.cloned.1.call-done = bf16[64,2,8,128]{3,0,2,1:T(8,128)(2,1)} async-done(((bf16[64,2,8,128]{3,0,2,1:T(8,128)(2,1)}), bf16[64,2,8,128]{3,0,2,1:T(8,128)(2,1)}) %all-reduce.3.cloned.1.call-update) | async-done | bytes 262160
  226.4 4.6 %all-gather.2 = bf16[128,1,2,128]{3,0,2,1:T(8,128)(2,1)S(1)} all-gather(bf16[64,1,2,128]{3,0,2,1:T(8,128)(2,1)S(1)} %get-tuple-element.347), channel_id=4, replica_groups=mesh['img'=4,'seq'=2,'tp'=4] {'seq'}, dimensions={0}, use_global_device_ids=true | all-gather | bytes 98304 | tf_op jit(solution)/shard_map/all_gather | solution.py:143
  231.0 4.8 %all-gather.3 = bf16[128,1,2,128]{3,0,2,1:T(8,128)(2,1)S(1)} all-gather(bf16[64,1,2,128]{3,0,2,1:T(8,128)(2,1)S(1)} %get-tuple-element.346), channel_id=5, replica_groups=mesh['img'=4,'seq'=2,'tp'=4] {'seq'}, dimensions={0}, use_global_device_ids=true | all-gather | bytes 98304 | tf_op jit(solution)/shard_map/all_gather | solution.py:144
  235.8 20.3 %while.32 = (s32[]{:T(128)}, f32[2,8,512]{2,1,0:T(8,128)S(1)}, f32[2,8,512]{2,1,0:T(8,128)S(1)}, f32[2,8,512,128]{3,2,1,0:T(8,128)}, s32[2]{0:T(128)S(1)}, /*ind...) while((s32[]{:T(128)}, f32[2,8,512]{2,1,0:T(8,128)S(1)}, ...), condition=%wide.region_14.15_spmd, body=%wide.region_11.14_spmd.sunk | while | flops 277364864 | bytes 50923320 | solution.py:162
  240.4 3.6 %multiply_add_fusion.5 = f32[2,8,512,128]{3,2,1,0:T(8,128)S(1)} fusion(f32[2,8,512,128]{3,2,1,0:T(8,128)S(1)} %copy-done.2, f32[2,8,512]{2,1,0:T(8,128)S(1)} %get-tuple-element.466, f32[2,64,512,8]{2,1,3,0:T(8,128)S(1)} %get-tuple-element.464, f32[2,8,512]{2,1,0:T(8,128)S(1)} %max.14, pred[64]{0:T(512)(128)(4,1)S(1)} %add_compare_fusion.3, ...), kind=kOutput, calls=%fused_computation.clone.1 | convolution fusion | flops 138936320 | bytes 10585092 | tf_op jit(solution)/shard_map/while/body/eval_jaxpr/kgcn,nkd->kgcd/dot_general | solution.py:25
  250.5 3.6 %multiply_add_fusion.5 = f32[2,8,512,128]{3,2,1,0:T(8,128)S(1)} fusion(f32[2,8,512,128]{3,2,1,0:T(8,128)S(1)} %copy-done.2, f32[2,8,512]{2,1,0:T(8,128)S(1)} %get-tuple-element.466, f32[2,64,512,8]{2,1,3,0:T(8,128)S(1)} %get-tuple-element.464, f32[2,8,512]{2,1,0:T(8,128)S(1)} %max.14, pred[64]{0:T(512)(128)(4,1)S(1)} %add_compare_fusion.3, ...), kind=kOutput, calls=%fused_computation.clone.1 | convolution fusion | flops 138936320 | bytes 10585092 | tf_op jit(solution)/shard_map/while/body/eval_jaxpr/kgcn,nkd->kgcd/dot_general | solution.py:25
  256.1 3.0 %fusion.45 = bf16[512,2,8,128]{3,0,2,1:T(8,128)(2,1)S(1)} fusion(f32[2,8,512,128]{3,2,1,0:T(8,128)} %get-tuple-element.211, f32[2,8,512]{2,1,0:T(8,128)S(1)} %get-tuple-element.212), kind=kLoop, calls=%fused_computation.74 | loop fusion | flops 2097152 | bytes 6324224 | tf_op jit(solution)/shard_map/convert_element_type | solution.py:165
  259.1 2.7 copy.95
  (121 shorter events, 80.6 us)
Async XLA Ops:
  6.5 126.6 %copy-start = (bf16[1280,1280]{1,0:T(8,128)(2,1)S(1)}, bf16[1280,1280]{1,0:T(8,128)(2,1)}, u32[]{:S(2)}) copy-start(bf16[1280,1280]{1,0:T(8,128)(2,1)} %param.15) | copy-start | bytes 9830404
  6.5 143.3 %all-gather.7.cloned.1.call-start = ((), (), s32[]{:S(2)}) async-start(), calls=%async_computation.2 | async-start | bytes 23592960 | tf_op jit(solution)/shard_map/all_gather | solution.py:105
  7.3 176.8 %all-gather.9.cloned.1.call-start = ((), (), s32[]{:S(2)}) async-start(), calls=%async_computation.3 | async-start | bytes 9437184 | tf_op jit(solution)/shard_map/all_gather | solution.py:116
  13.1 22.4 %all-to-all-start = ((bf16[64,3,16,80]{3,0,1,2:T(8,128)(2,1)}), bf16[64,3,16,80]{3,0,1,2:T(8,128)(2,1)}, u32[]{:S(2)}, u32[]{:S(2)}) async-start(bf16[64,3,16,80]{3,0,1,2:T(8,128)(2,1)} %copy.59), calls=%async_computation | async-start | bytes 1572864 | tf_op jit(solution)/shard_map/all_to_all | solution.py:49
  17.4 2.7 %copy-start.8 = (bf16[1,512,2,2,128]{4,3,2,1,0:T(2,128)(2,1)S(1)}, bf16[1,512,2,2,128]{4,3,2,1,0:T(2,128)(2,1)}, u32[]{:S(2)}) copy-start(bf16[1,512,2,2,128]{4,3,2,1,0:T(2,128)(2,1)} %param.21) | copy-start | bytes 1572868
  20.0 4.4 %copy-start.4 = (bf16[1,512,16,128]{3,1,2,0:T(8,128)(2,1)}, bf16[1,512,16,128]{3,1,2,0:T(8,128)(2,1)S(1)}, u32[]{:S(2)}) copy-start(bf16[1,512,16,128]{3,1,2,0:T(8,128)(2,1)S(1)} %copy.56) | copy-start | bytes 6291460
  20.1 4.3 %copy-start.6 = (pred[512,512]{0,1:T(8,128)(4,1)}, pred[512,512]{0,1:T(8,128)(4,1)S(1)}, u32[]{:S(2)}) copy-start(pred[512,512]{0,1:T(8,128)(4,1)S(1)} %iota_compare_fusion) | copy-start | bytes 786436
  24.4 5.8 %copy-start.5 = (f32[2,512,512,8]{2,1,3,0:T(8,128)}, f32[2,512,512,8]{2,1,3,0:T(8,128)S(1)}, u32[]{:S(2)}) copy-start(f32[2,512,512,8]{2,1,3,0:T(8,128)S(1)} %get-tuple-element.351) | copy-start | bytes 50331652
  116.8 17.4 %copy-start.11 = (f32[1280]{0:T(1024)S(1)}, f32[1280]{0:T(1024)}, u32[]{:S(2)}) copy-start(f32[1280]{0:T(1024)} %param.16) | copy-start | bytes 15364
  120.8 9.4 %all-to-all-start.1 = ((bf16[128,8,80]{2,1,0:T(8,128)(2,1)}), bf16[128,8,80]{2,1,0:T(8,128)(2,1)}, u32[]{:S(2)}, u32[]{:S(2)}) async-start(bf16[128,8,80]{2,1,0:T(8,128)(2,1)} %fusion.56), calls=%async_computation.1 | async-start | bytes 524288 | tf_op jit(solution)/shard_map/all_to_all | solution.py:85
  124.9 100.8 %all-reduce.3.cloned.1.call-start = ((), (), s32[]{:S(2)}) async-start(), calls=%async_computation.4 | async-start | bytes 524288
  149.8 34.2 %copy-start.10 = (f32[2048]{0:T(1024)S(1)}, f32[2048]{0:T(1024)}, u32[]{:S(2)}) copy-start(f32[2048]{0:T(1024)} %param.18) | copy-start | bytes 24580
  168.2 21.7 %copy-start.7 = (pred[512,512]{0,1:T(8,128)(4,1)S(1)}, pred[512,512]{0,1:T(8,128)(4,1)}, u32[]{:S(2)}) copy-start(pred[512,512]{0,1:T(8,128)(4,1)} %copy-done.6) | copy-start | bytes 786436
  168.2 21.7 %copy-start.9 = (bf16[1,512,1,2,128]{4,3,2,1,0:T(2,128)(2,1)S(1)}, bf16[1,512,1,2,128]{4,3,2,1,0:T(2,128)(2,1)}, u32[]{:S(2)}) copy-start(bf16[1,512,1,2,128]{4,3,2,1,0:T(2,128)(2,1)} %get-tuple-element.344) | copy-start | bytes 786436
  189.9 10.5 %copy-start.12 = (u32[32]{0:T(128)S(1)}, u32[32]{0:T(128)}, u32[]{:S(2)}) copy-start(u32[32]{0:T(128)} %constant.207) | copy-start | bytes 388
  235.8 4.6 %copy-start.2 = (f32[2,8,512,128]{3,2,1,0:T(8,128)S(1)}, f32[2,8,512,128]{3,2,1,0:T(8,128)}, u32[]{:S(2)}) copy-start(f32[2,8,512,128]{3,2,1,0:T(8,128)} %get-tuple-element.526) | copy-start | bytes 12582916 | tf_op jit(solution)/shard_map/while
  244.0 1.9 copy-start.3
  245.9 4.6 %copy-start.2 = (f32[2,8,512,128]{3,2,1,0:T(8,128)S(1)}, f32[2,8,512,128]{3,2,1,0:T(8,128)}, u32[]{:S(2)}) copy-start(f32[2,8,512,128]{3,2,1,0:T(8,128)} %get-tuple-element.526) | copy-start | bytes 12582916 | tf_op jit(solution)/shard_map/while
  254.1 1.9 copy-start.3
  256.1 5.7 %copy-start.1 = (bf16[1280,1280]{1,0:T(8,128)(2,1)S(1)}, bf16[1280,1280]{1,0:T(8,128)(2,1)}, u32[]{:S(2)}) copy-start(bf16[1280,1280]{1,0:T(8,128)(2,1)} %param.15) | copy-start | bytes 9830404
Sparse Core Ops, SparseCore 0:
  9.2 115.9 all-gather.6
  127.1 56.9 all-gather.8
  190.0 35.5 all-reduce.2
where the time goes:
time: 270 us; the launch traced here: 268 us
  blocking collectives  67.6 us (25%)
  matrix products  58.1 us (22%)
  waiting for transfers between devices  50.5 us (19%)
  local copies, waits for them, and re-layouts  45.6 us (17%)
  other arithmetic  23.2 us (9%)
  between operations  14.7 us (5%)
  starting transfers between devices  8.49 us (3%)
    dot_general x7, matrix products, fold_block(): jnp.einsum(forms, weights.astype(jnp.bfloat16), value_block, preferred_el...  26.7 us
    unnamed x4, waiting for transfers between devices  25.4 us
    all_gather x1, blocking collectives, local(): key_piece = lax.all_gather(spread[:, 1], 'tp', axis=0, tiled=True)  17.9 us
    all_gather x1, blocking collectives, local(): value_piece = lax.all_gather(spread[:, 2], 'tp', axis=0, tiled=True)  16.4 us
    all_gather x1, waiting for transfers between devices, local(): lax.all_gather(kv_weight, ('img', 'seq'), axis=1, tiled=True)  15.8 us
    all_gather x1, blocking collectives, local(): token_rows = lax.all_gather(merged_local, 'tp', axis=0, tiled=True)  15.5 us
    unnamed x28, local copies, waits for them, and re-layouts  10.2 us
    reduce_sum x7, other arithmetic, fold_block(): weight_sum = weight_sum * decay + jnp.sum(weights, axis=-1)  9.87 us
  transfers between devices with their start and end apart: 5, of which 4 were waited for; matrix products, arithmetic and copies ran while one was open for 35% of the time, Pallas kernels for 0%

commit v1 on v0

--- a/solution.py
+++ b/solution.py
@@ -1,6 +1,7 @@
 import jax
 import jax.numpy as jnp
 from jax import lax
+from jax.sharding import Mesh
 from jax.sharding import PartitionSpec as P
 
 VIT_D = 1280
@@ -165,18 +166,231 @@
     return result.reshape(span_rows, kv_local * groups, HD).astype(jnp.bfloat16)[None]
 
 
+def swap_pairs(plane, seqs, tps, move):
+    pairs = []
+    for x in range(plane):
+        for c in range(2):
+            for s in range(seqs):
+                for t in range(tps):
+                    x2, c2, s2 = move(x, c, s)
+                    pairs.append((((x * 2 + c) * seqs + s) * tps + t, ((x2 * 2 + c2) * seqs + s2) * tps + t))
+    return pairs
+
+
+def fast_local(
+    vit_qkv,
+    patch_counts,
+    vit_out_weight,
+    vit_norm_gain,
+    merger_weight,
+    lm_norm_gain,
+    kv_weight,
+    queries,
+    span_kv,
+):
+    everything = ("x", "c", "seq", "tp")
+    plane = lax.axis_size("x")
+    seqs = lax.axis_size("seq")
+    tps = lax.axis_size("tp")
+    x, c, s, t = (lax.axis_index(name) for name in everything)
+    owners = seqs * tps
+    patch_rows = vit_qkv.shape[1]
+    token_rows = patch_rows // 4
+    patch_total = patch_counts[0]
+    share = VIT_D // owners
+    heads = VIT_HEADS // owners
+
+    def swap(value, move):
+        return lax.ppermute(value, everything, swap_pairs(plane, seqs, tps, move))
+
+    def other_core(x, c, s):
+        return x, 1 - c, s
+
+    def first_hop(x, c, s):
+        return (1 - x, c, s) if c == 0 else (x, c, 1 - s)
+
+    def second_hop(x, c, s):
+        return (x, c, 1 - s) if c == 0 else (1 - x, c, s)
+
+    other_rows = swap(merger_weight, other_core)
+    kv_one = kv_weight[None]
+    kv_hop = swap(kv_one, first_hop)
+    kv_two = jnp.concatenate([kv_one, kv_hop])
+    kv_far = swap(kv_two, second_hop)
+    kv_four = jnp.concatenate([kv_two, kv_far])
+    kv_other = swap(kv_four, other_core)
+
+    packed = vit_qkv[0].reshape(patch_rows, 3, owners, share)
+    packed = jnp.transpose(packed, (2, 0, 1, 3)).reshape(owners, patch_rows, 3 * share)
+    spread = lax.all_to_all(packed, ("seq", "tp"), split_axis=0, concat_axis=0, tiled=True)
+    patches = owners * patch_rows
+    spread = spread.reshape(patches, 3, heads, VIT_HDIM)
+    scores = jnp.einsum(
+        "qhd,khd->hqk", spread[:, 0], spread[:, 1], preferred_element_type=jnp.float32
+    ) * VIT_HDIM ** (-0.5)
+    usable = jnp.arange(patches, dtype=jnp.int32) < patch_total
+    scores = jnp.where(usable, scores, masked_score)
+    weights = jnp.exp(scores - jnp.max(scores, axis=-1, keepdims=True))
+    weight_sum = jnp.sum(weights, axis=-1)
+    blended = jnp.einsum(
+        "hqk,khd->qhd", weights.astype(jnp.bfloat16), spread[:, 2], preferred_element_type=jnp.float32
+    )
+    blended = blended / weight_sum.T[..., None]
+    attended = blended.astype(jnp.bfloat16).reshape(owners, patch_rows, share)
+    attended = lax.all_to_all(attended, ("seq", "tp"), split_axis=0, concat_axis=0, tiled=True)
+    attended = jnp.transpose(attended, (1, 0, 2)).reshape(patch_rows, VIT_D)
+
+    hidden = jnp.dot(attended, vit_out_weight, preferred_element_type=jnp.float32)
+    patch_ids = (s * tps + t) * patch_rows + jnp.arange(patch_rows, dtype=jnp.int32)
+    hidden = jnp.where((patch_ids < patch_total)[:, None], hidden, 0.0)
+    centred = hidden - jnp.mean(hidden, axis=-1, keepdims=True)
+    spread_sq = jnp.mean(centred * centred, axis=-1, keepdims=True)
+    normed = (centred * lax.rsqrt(spread_sq + 1e-06) * vit_norm_gain).astype(jnp.bfloat16)
+
+    rows_local = merger_weight.shape[0]
+    merged = normed.reshape(token_rows, plane, 2, seqs, rows_local)
+    merged = jnp.where(c == 0, merged, merged[:, :, ::-1])
+    merged = jnp.transpose(merged, (1, 3, 0, 2, 4)).reshape(plane, seqs, 1, token_rows, 2 * rows_local)
+    merged = jnp.broadcast_to(merged, (plane, seqs, tps, token_rows, 2 * rows_local))
+    merged = merged.reshape(plane * owners, token_rows, 2 * rows_local)
+    tokens = lax.all_to_all(merged, ("x", "seq", "tp"), split_axis=0, concat_axis=0, tiled=True)
+    half = tps * token_rows
+    tokens = tokens.reshape(plane * seqs, half, 2 * rows_local)
+
+    def quarter(xq, sq):
+        return xq * seqs + sq
+
+    far = quarter(1 - x, 1 - s)
+    order = jnp.where(
+        c == 0,
+        jnp.stack([far, quarter(1 - x, s), quarter(x, 1 - s), quarter(x, s)]),
+        jnp.stack([far, quarter(x, 1 - s), quarter(1 - x, s), quarter(x, s)]),
+    )
+    tokens = jnp.concatenate(
+        [lax.dynamic_slice_in_dim(tokens, order[k], 1, 0) for k in range(4)]
+    ).reshape(4 * half, 2 * rows_local)
+    partial = jnp.dot(tokens[:, :rows_local], merger_weight, preferred_element_type=jnp.float32)
+    partial = partial + jnp.dot(
+        tokens[:, rows_local:], other_rows, preferred_element_type=jnp.float32
+    )
+    sent = partial[: 2 * half].astype(jnp.bfloat16)
+    kept = partial[2 * half :] + swap(sent, first_hop).astype(jnp.float32)
+    sent = kept[:half].astype(jnp.bfloat16)
+    embedded = kept[half:] + swap(sent, second_hop).astype(jnp.float32)
+
+    squares = jnp.sum(embedded * embedded, axis=-1)
+    gained = (embedded * lm_norm_gain).astype(jnp.bfloat16)
+
+    def project(block):
+        return jnp.dot(gained, block, preferred_element_type=jnp.float32).astype(jnp.bfloat16)
+
+    columns = []
+    for core_step in range(2):
+        for far_step in range(2):
+            for hop_step in range(2):
+                bank = kv_other if core_step else kv_four
+                columns.append(project(bank[far_step * 2 + hop_step]))
+    stacked = jnp.stack(columns)
+    slots = []
+    for kind in range(2):
+        for dest in range(tps):
+            block_c, block_s = dest // seqs, dest % seqs
+            dx = x ^ kind
+            ds = s ^ block_s
+            dc = c ^ block_c
+            owner_core = block_c
+            hop = jnp.where(owner_core == 0, dx, ds)
+            fars = jnp.where(owner_core == 0, ds, dx)
+            slots.append((dc * 2 + fars) * 2 + hop)
+    placed = jnp.stack([lax.dynamic_index_in_dim(stacked, k, 0, False) for k in slots])
+    placed = placed.reshape(2, tps, half, -1)
+    payload = jnp.concatenate([placed[0], placed[1]], axis=-1)
+    coarse = squares.astype(jnp.bfloat16)
+    fine = (squares - coarse.astype(jnp.float32)).astype(jnp.bfloat16)
+    lane = jnp.arange(128, dtype=jnp.int32)
+    extra = jnp.where(lane == 0, coarse[:, None], jnp.where(lane == 1, fine[:, None], 0))
+    extra = jnp.broadcast_to(extra.astype(jnp.bfloat16)[None], (tps, half, 128))
+    payload = jnp.concatenate([payload, extra], axis=-1)
+    sums = lax.all_to_all(payload, "tp", split_axis=0, concat_axis=0, tiled=True)
+    sums = jnp.sum(sums.astype(jnp.float32), axis=0)
+    width = placed.shape[-1]
+    total = sums[:, 2 * width] + sums[:, 2 * width + 1]
+    visual = sums[:, : 2 * width] * lax.rsqrt(total / D + 1e-06)[:, None]
+    visual = visual.astype(jnp.bfloat16)
+    twin = swap(visual, lambda x, c, s: (x, c, 1 - s))
+    first = jnp.where(s == 0, visual, twin)
+    second = jnp.where(s == 0, twin, visual)
+    visual = jnp.concatenate([first, second]).reshape(2 * half, 2, -1, HD)
+
+    span_rows = queries.shape[1]
+    kv_local = span_kv.shape[3]
+    groups = HQ // KVH
+    lm_scaling = HD ** (-0.5)
+    grouped = queries[0].reshape(span_rows, kv_local, groups, HD)
+    causal = jnp.arange(span_rows)[:, None] >= jnp.arange(span_rows)[None, :]
+    near_scores = (
+        jnp.einsum("ckgd,nkd->kgcn", grouped, span_kv[0, :, 0], preferred_element_type=jnp.float32)
+        * lm_scaling
+    )
+    initial = (
+        jnp.full((kv_local, groups, span_rows), masked_score, jnp.float32),
+        jnp.zeros((kv_local, groups, span_rows), jnp.float32),
+        jnp.zeros((kv_local, groups, span_rows, HD), jnp.float32),
+    )
+    state = fold_block(
+        initial, near_scores, causal[None, None], span_kv[0, :, 1], "kgcn,nkd->kgcd"
+    )
+    seen = jnp.arange(2 * half, dtype=jnp.int32) < patch_total // 4
+    far_scores = (
+        jnp.einsum("ckgd,nkd->kgcn", grouped, visual[:, 0], preferred_element_type=jnp.float32)
+        * lm_scaling
+    )
+    state = fold_block(state, far_scores, seen[None, None, None], visual[:, 1], "kgcn,nkd->kgcd")
+    peak, weight_sum, blended = state
+    result = jnp.transpose(blended / weight_sum[..., None], (2, 0, 1, 3))
+    return result.reshape(span_rows, kv_local * groups, HD).astype(jnp.bfloat16)[None]
+
+
 def solution(mesh):
+    sizes = dict(mesh.shape)
+    images, seqs, tps = (sizes[name] for name in ("img", "seq", "tp"))
+    suited = (
+        images == 4
+        and seqs == 2
+        and images * seqs == 2 * tps
+        and VIT_HEADS % (seqs * tps) == 0
+        and KVH % tps == 0
+    )
+    if not suited:
+        placed = (
+            P("img", ("seq", "tp"), None, None),
+            P("img"),
+            P(),
+            P(),
+            P(("img", "seq"), "tp"),
+            P("tp"),
+            P("tp", ("img", "seq")),
+            P("img", "seq", "tp", None),
+            P("img", "seq", None, "tp", None),
+        )
+        return jax.shard_map(
+            local, mesh=mesh, in_specs=placed, out_specs=P("img", "seq", "tp", None), check_vma=False
+        )
+    split = Mesh(
+        mesh.devices.reshape(images // 2, 2, seqs, tps), ("x", "c", "seq", "tp")
+    )
+    image = ("x", "c")
     placed = (
-        P("img", ("seq", "tp"), None, None),
-        P("img"),
+        P(image, ("seq", "tp"), None, None),
+        P(image),
         P(),
         P(),
-        P(("img", "seq"), "tp"),
+        P(("x", "c", "seq"), "tp"),
         P("tp"),
-        P("tp", ("img", "seq")),
-        P("img", "seq", "tp", None),
-        P("img", "seq", None, "tp", None),
+        P("tp", ("x", "c", "seq")),
+        P(image, "seq", "tp", None),
+        P(image, "seq", None, "tp", None),
     )
     return jax.shard_map(
-        local, mesh=mesh, in_specs=placed, out_specs=P("img", "seq", "tp", None), check_vma=False
-    )
+        fast_local, mesh=split, in_specs=placed, out_specs=P(image, "seq", "tp", None), check_vma=False
+    )

time: 270 us -> 167 us (0.62)
  blocking collectives: 67.6 us -> 0 us
  matrix products: 58.1 us -> 38.7 us
  starting transfers between devices: 8.49 us -> 27.1 us
  local copies, waits for them, and re-layouts: 45.6 us -> 33.8 us
  waiting for transfers between devices: 50.5 us -> 42.3 us
  other arithmetic: 23.2 us -> 15.6 us
  between operations: 14.7 us -> 8.63 us
    all_gather x5 -> x0, blocking collectives: 59.1 us -> none  [the longest x1 17.9 us: local(): key_piece = lax.all_gather(spread[:, 1], 'tp', axis=0, tiled=True)]
    unnamed x4 -> x0, waiting for transfers between devices: 25.4 us -> none
    ppermute x0 -> x7, waiting for transfers between devices: none -> 23.5 us  [swap(): return lax.ppermute(value, everything, swap_pairs(plane, seqs, tps, move))]
    dot_general x7 -> x2, matrix products: 26.7 us -> 9.9 us  [fold_block(): jnp.einsum(forms, weights.astype(jnp.bfloat16), value_block, preferred_el...]
    all_gather x2 -> x0, waiting for transfers between devices: 15.8 us -> none  [the longest x1 15.8 us: local(): lax.all_gather(kv_weight, ('img', 'seq'), axis=1, tiled=True)]
    all_to_all x2 -> x4, starting transfers between devices: 8.41 us -> 18.8 us  [the longest x1 7.31 us: fast_local(): lax.all_to_all(packed, ('seq', 'tp'), split_axis=0, concat_axis=0, tiled=...]
    all_to_all x2 -> x4, waiting for transfers between devices: 9.24 us -> 18.8 us  [the longest x1 13.4 us: fast_local(): lax.all_to_all(packed, ('seq', 'tp'), split_axis=0, concat_axis=0, tiled=...]
    psum x1 -> x0, blocking collectives: 8.5 us -> none  [local(): lax.psum(jnp.sum(embedded_wide * embedded_wide, axis=-1), 'tp')]
  transfers between devices with their start and end apart: 5 -> 11, of which waited for: 4 -> 7; matrix products, arithmetic and copies ran while one was open for 35% -> 30% of each run, Pallas kernels for 0% -> 0%
where the time goes in v1:
time: 167 us; the launch traced here: 166 us
  waiting for transfers between devices  42.3 us (25%)
  matrix products  38.7 us (23%)
  local copies, waits for them, and re-layouts  33.8 us (20%)
  starting transfers between devices  27.1 us (16%)
  other arithmetic  15.6 us (9%)
  between operations  8.63 us (5%)
    ppermute x7, waiting for transfers between devices, swap(): return lax.ppermute(value, everything, swap_pairs(plane, seqs, tps, move))  23.5 us
    all_to_all x1, waiting for transfers between devices, fast_local(): lax.all_to_all(packed, ('seq', 'tp'), split_axis=0, concat_axis=0, tiled=...  13.4 us
    dot_general x8, matrix products, project(): jnp.dot(gained, block, preferred_element_type=jnp.float32)  11.1 us
    dot_general x2, matrix products, fold_block(): jnp.einsum(forms, weights.astype(jnp.bfloat16), value_block, preferred_el...  9.9 us
    ppermute x7, starting transfers between devices, swap(): return lax.ppermute(value, everything, swap_pairs(plane, seqs, tps, move))  8.27 us
    dot_general x1, matrix products, fast_local(): jnp.einsum('ckgd,nkd->kgcn', grouped, span_kv[0, :, 0], preferred_element...  7.49 us
    all_to_all x1, starting transfers between devices, fast_local(): lax.all_to_all(packed, ('seq', 'tp'), split_axis=0, concat_axis=0, tiled=...  7.31 us
    unnamed x23, local copies, waits for them, and re-layouts  6.65 us
  transfers between devices with their start and end apart: 11, of which 7 were waited for; matrix products, arithmetic and copies ran while one was open for 30% of the time, Pallas kernels for 0%

profile of v1, /device:TPU:0, one launch (start us, length us, event | category | flops | bytes accessed | tf_op | source)
XLA Modules:
  0.0 166.1 jit_solution(16427002330109263701)
XLA Ops:
  0.0 2.9 %reshape_squeeze.7 = bf16[64,3,8,160]{3,2,0,1:T(8,128)(2,1)} reshape(bf16[1,64,3,1280]{3,1,2,0:T(8,128)(2,1)} %param.9) | data formatting | bytes 983040 | tf_op jit(solution)/shard_map/reshape;squeeze | solution.py:223
  2.9 2.8 %copy.121 = bf16[64,3,8,160]{3,1,0,2:T(4,128)(2,1)} copy(bf16[64,3,8,160]{3,2,0,1:T(8,128)(2,1)} %reshape_squeeze.7) | data formatting | bytes 983040 | tf_op jit(solution)/shard_map/reshape;squeeze | solution.py:223
  5.7 3.2 %reshape.173 = bf16[8,64,480]{2,1,0:T(8,128)(2,1)} reshape(bf16[8,64,3,160]{3,2,1,0:T(4,128)(2,1)} %bitcast.215) | data formatting | bytes 983040 | tf_op jit(solution)/shard_map/reshape | solution.py:224
  8.9 7.3 %all-to-all-start = ((bf16[8,64,480]{2,1,0:T(8,128)(2,1)}), bf16[8,64,480]{2,1,0:T(8,128)(2,1)}, u32[]{:S(2)}, u32[]{:S(2)}) async-start(bf16[8,64,480]{2,1,0:T(8,128)(2,1)} %reshape.173), calls=%async_computation | async-start | bytes 1048576 | tf_op jit(solution)/shard_map/all_to_all | solution.py:225
  18.4 13.4 %all-to-all-done = bf16[8,64,480]{2,1,0:T(8,128)(2,1)} async-done(((bf16[8,64,480]{2,1,0:T(8,128)(2,1)}), bf16[8,64,480]{2,1,0:T(8,128)(2,1)}, u32[]{:S(2)}, u32[]{:S(2)}) %all-to-all-start) | async-done | bytes 491552 | tf_op jit(solution)/shard_map/all_to_all | solution.py:225
  31.8 3.1 %reshape.174 = bf16[512,3,2,80]{3,2,1,0:T(2,128)(2,1)} reshape(bf16[8,64,480]{2,1,0:T(8,128)(2,1)} %all-to-all-done) | data formatting | bytes 983040 | tf_op jit(solution)/shard_map/reshape | solution.py:227
  34.9 2.4 %fusion.80 = (bf16[512,1,2,80]{3,2,1,0:T(2,128)(2,1)S(1)}, bf16[512,1,2,80]{3,2,1,0:T(2,128)(2,1)}, bf16[512,1,2,80]{3,2,1,0:T(2,128)(2,1)}) fusion(bf16[512,3,2,80]{3,2,1,0:T(2,128)(2,1)} %reshape.174), kind=kLoop, calls=%fused_computation.152 | loop fusion | bytes 983040 | tf_op jit(solution)/shard_map/slice | solution.py:236
  47.3 3.4 %all-to-all-start.1 = ((bf16[8,64,160]{2,1,0:T(8,128)(2,1)}), bf16[8,64,160]{2,1,0:T(8,128)(2,1)S(1)}, u32[]{:S(2)}, u32[]{:S(2)}) async-start(bf16[8,64,160]{2,1,0:T(8,128)(2,1)} %copy.81), calls=%async_computation.1 | async-start | bytes 524288 | tf_op jit(solution)/shard_map/all_to_all | solution.py:240
  50.8 3.1 %pad_maximum_fusion.1 = bf16[2,2048,256]{2,1,0:T(8,128)(2,1)} fusion(bf16[1,2048,256]{2,1,0:T(8,128)(2,1)} %collective-permute-done.3, bf16[1,2048,256]{2,1,0:T(8,128)(2,1)} %bitcast.211), kind=kLoop, calls=%fused_computation.23 | loop fusion | flops 1048576 | bytes 4194304 | tf_op jit(solution)/shard_map/concatenate | solution.py:218
  55.8 3.7 %all-to-all-done.1 = bf16[8,64,160]{2,1,0:T(8,128)(2,1)S(1)} async-done(((bf16[8,64,160]{2,1,0:T(8,128)(2,1)}), bf16[8,64,160]{2,1,0:T(8,128)(2,1)S(1)}, u32[]{:S(2)}, u32[]{:S(2)}) %all-to-all-start.1) | async-done | bytes 163872 | tf_op jit(solution)/shard_map/all_to_all | solution.py:240
  65.0 3.8 %all-to-all-start.2 = ((bf16[16,16,1280]{2,1,0:T(8,128)(2,1)}), bf16[16,16,1280]{2,1,0:T(8,128)(2,1)S(1)}, u32[]{:S(2)}, u32[]{:S(2)}) async-start(bf16[16,16,1280]{2,1,0:T(8,128)(2,1)} %bitcast.19), calls=%async_computation.2 | async-start | bytes 1310720 | tf_op jit(solution)/shard_map/all_to_all | solution.py:256
  77.1 10.4 %collective-permute-done.4 = bf16[2,2048,256]{2,1,0:T(8,128)(2,1)} collective-permute-done((bf16[2,2048,256]{2,1,0:T(8,128)(2,1)}, bf16[2,2048,256]{2,1,0:T(8,128)(2,1)}, u32[]{:S(2)}, u32[]{:S(2)}) %collective-permute-start.4) | collective-permute-done | bytes 2097184 | tf_op jit(solution)/shard_map/ppermute | solution.py:204
  87.5 3.5 %pad_maximum_fusion = bf16[4,2048,256]{2,1,0:T(8,128)(2,1)} fusion(bf16[2,2048,256]{2,1,0:T(8,128)(2,1)} %collective-permute-done.4, bf16[1,2048,256]{2,1,0:T(8,128)(2,1)} %collective-permute-done.3, bf16[1,2048,256]{2,1,0:T(8,128)(2,1)S(1)} %bitcast.212), kind=kLoop, calls=%fused_computation.7 | loop fusion | flops 4194304 | bytes 8388608 | tf_op jit(solution)/shard_map/concatenate | solution.py:220
  91.1 2.7 %fusion.54 = f32[256,2048]{1,0:T(8,128)S(1)} fusion(bf16[640,2048]{1,0:T(8,128)(2,1)} %param.13, bf16[256,1280]{1,0:T(8,128)(2,1)S(1)} %bitcast.216), kind=kOutput, calls=%fused_computation.87 | convolution fusion | flops 671088640 | bytes 5046272 | tf_op jit(solution)/shard_map/dot_general | solution.py:272
  93.9 2.7 %convolution_add_fusion = f32[256,2048]{1,0:T(8,128)S(1)} fusion(f32[256,2048]{1,0:T(8,128)S(1)} %fusion.54, bf16[640,2048]{1,0:T(8,128)(2,1)} %collective-permute-done, bf16[256,1280]{1,0:T(8,128)(2,1)S(1)} %bitcast.217), kind=kOutput, calls=%fused_computation.20 | convolution fusion | flops 671612928 | bytes 7143424 | tf_op jit(solution)/shard_map/dot_general | solution.py:273
  98.3 7.6 %collective-permute-done.1 = bf16[128,2048]{1,0:T(8,128)(2,1)S(1)} collective-permute-done((bf16[128,2048]{1,0:T(8,128)(2,1)S(1)}, bf16[128,2048]{1,0:T(8,128)(2,1)S(1)}, u32[]{:S(2)}, u32[]{:S(2)}) %collective-permute-start.1) | collective-permute-done | bytes 524320 | tf_op jit(solution)/shard_map/ppermute | solution.py:204
  108.8 2.1 %fusion.81 = (bf16[1,512,1,2,128]{4,3,2,1,0:T(2,128)(2,1)}, bf16[1,512,1,2,128]{4,3,2,1,0:T(2,128)(2,1)S(1)}) fusion(bf16[1,512,2,2,128]{4,3,2,1,0:T(2,128)(2,1)} %param.17), kind=kLoop, calls=%fused_computation.153 | loop fusion | bytes 1048576 | tf_op jit(solution)/shard_map/slice | solution.py:341
  110.8 2.7 %collective-permute-done.2 = bf16[64,2048]{1,0:T(8,128)(2,1)S(1)} collective-permute-done((bf16[64,2048]{1,0:T(8,128)(2,1)S(1)}, bf16[64,2048]{1,0:T(8,128)(2,1)S(1)}, u32[]{:S(2)}, u32[]{:S(2)}) %collective-permute-start.2) | collective-permute-done | bytes 262176 | tf_op jit(solution)/shard_map/ppermute | solution.py:204
  126.8 4.3 %all-to-all-start.3 = ((bf16[4,64,640]{2,1,0:T(8,128)(2,1)}), bf16[4,64,640]{2,1,0:T(8,128)(2,1)S(1)}, u32[]{:S(2)}, u32[]{:S(2)}) async-start(bf16[4,64,640]{2,1,0:T(8,128)(2,1)} %pad_maximum_fusion.3), calls=%async_computation.3 | async-start | bytes 655360 | tf_op jit(solution)/shard_map/all_to_all | solution.py:314
  131.1 7.5 %fusion = (f32[2,8,512]{2,1,0:T(8,128)S(1)}, f32[2,512,512,8]{2,1,3,0:T(8,128)}) fusion(pred[512,512]{0,1:T(8,128)(4,1)S(1)} %iota_compare_fusion, bf16[512,2,8,128]{3,2,1,0:T(8,128)(2,1)S(1)} %bitcast.213, bf16[1,512,1,2,128]{4,3,2,1,0:T(2,128)(2,1)S(1)} %get-tuple-element.17), kind=kOutput, calls=%fused_computation.2 | convolution fusion | flops 1086316544 | bytes 19431424 | tf_op jit(solution)/shard_map/ckgd,nkd->kgcn/dot_general | solution.py:332
  142.2 2.8 %collective-permute-done.6 = bf16[64,512]{1,0:T(8,128)(2,1)S(1)} collective-permute-done((bf16[64,512]{1,0:T(8,128)(2,1)S(1)}, bf16[64,512]{1,0:T(8,128)(2,1)S(1)}, u32[]{:S(2)}, u32[]{:S(2)}) %collective-permute-start.6) | collective-permute-done | bytes 65568 | tf_op jit(solution)/shard_map/ppermute | solution.py:204
  151.0 4.0 %fusion.1 = f32[2,8,512]{2,1,0:T(8,128)S(1)} fusion(f32[2,512,512,8]{2,1,3,0:T(8,128)S(1)} %copy-done.2, f32[2,8,512]{2,1,0:T(8,128)S(1)} %get-tuple-element.29, pred[512,512]{0,1:T(8,128)(4,1)S(1)} %iota_compare_fusion), kind=kLoop, calls=%fused_computation.3 | loop fusion | flops 20963328 | bytes 17104896 | tf_op jit(solution)/shard_map/reduce_sum | solution.py:25
  155.1 8.3 %fusion.7 = bf16[512,2,8,128]{3,0,2,1:T(8,128)(2,1)S(1)} fusion(f32[2,8,512,128]{3,2,1,0:T(8,128)S(1)} %fusion.15, f32[2,512,512,8]{2,1,3,0:T(8,128)S(1)} %copy-done.2, f32[2,8,512]{2,1,0:T(8,128)S(1)} %get-tuple-element.29, pred[512,512]{0,1:T(8,128)(4,1)S(1)} %iota_compare_fusion, f32[512,2,8]{0,2,1:T(8,128)S(1)} %get-tuple-element.5, ...), kind=kOutput, calls=%fused_computation.10 | convolution fusion | flops 1099956224 | bytes 23724032 | tf_op jit(solution)/shard_map/kgcn,nkd->kgcd/dot_general | solution.py:26
  163.4 2.7 %copy.90 = bf16[1,512,16,128]{3,2,1,0:T(8,128)(2,1)} copy(bf16[1,512,16,128]{3,1,2,0:T(8,128)(2,1)S(1)} %bitcast.219) | data formatting | bytes 4194304 | tf_op jit(solution)/shard_map/convert_element_type | solution.py:351
  (90 shorter events, 47.1 us)
Async XLA Ops:
  0.0 61.6 %copy-start = (bf16[1280,1280]{1,0:T(8,128)(2,1)S(1)}, bf16[1280,1280]{1,0:T(8,128)(2,1)}, u32[]{:S(2)}) copy-start(bf16[1280,1280]{1,0:T(8,128)(2,1)} %param.11) | copy-start | bytes 9830404
  8.9 22.9 %all-to-all-start = ((bf16[8,64,480]{2,1,0:T(8,128)(2,1)}), bf16[8,64,480]{2,1,0:T(8,128)(2,1)}, u32[]{:S(2)}, u32[]{:S(2)}) async-start(bf16[8,64,480]{2,1,0:T(8,128)(2,1)} %reshape.173), calls=%async_computation | async-start | bytes 1048576 | tf_op jit(solution)/shard_map/all_to_all | solution.py:225
  16.2 77.7 %collective-permute-start = (bf16[640,2048]{1,0:T(8,128)(2,1)}, bf16[640,2048]{1,0:T(8,128)(2,1)}, u32[]{:S(2)}, u32[]{:S(2)}) collective-permute-start(bf16[640,2048]{1,0:T(8,128)(2,1)} %param.13), channel_id=1, source_target_pairs={{0,8},{1,9},{2,10},{3,11},{4,12},{5,13},{6,14},{7,15},{8,0},{9,1},... | collective-permute-start | bytes 7864328 | tf_op jit(solution)/shard_map/ppermute | solution.py:204
  16.2 34.6 %collective-permute-start.3 = (bf16[1,2048,256]{2,1,0:T(8,128)(2,1)}, bf16[1,2048,256]{2,1,0:T(8,128)(2,1)}, u32[]{:S(2)}, u32[]{:S(2)}) collective-permute-start(bf16[1,2048,256]{2,1,0:T(8,128)(2,1)} %bitcast.210), channel_id=1, source_target_pairs={{0,16},{1,17},{2,18},{3,19},{4,20},{5,21},{6,22},{7,23},{8,12},{9,... | collective-permute-start | bytes 3145736 | tf_op jit(solution)/shard_map/ppermute | solution.py:204
  41.7 2.1 %copy-start.7 = (bf16[512,1,2,80]{0,3,2,1:T(8,128)(2,1)S(1)}, bf16[512,1,2,80]{0,3,2,1:T(8,128)(2,1)}, u32[]{:S(2)}) copy-start(bf16[512,1,2,80]{0,3,2,1:T(8,128)(2,1)} %copy.100) | copy-start | bytes 491524
  47.3 12.2 %all-to-all-start.1 = ((bf16[8,64,160]{2,1,0:T(8,128)(2,1)}), bf16[8,64,160]{2,1,0:T(8,128)(2,1)S(1)}, u32[]{:S(2)}, u32[]{:S(2)}) async-start(bf16[8,64,160]{2,1,0:T(8,128)(2,1)} %copy.81), calls=%async_computation.1 | async-start | bytes 524288 | tf_op jit(solution)/shard_map/all_to_all | solution.py:240
  50.8 11.8 %copy-start.8 = (f32[1280]{0:T(1024)S(1)}, f32[1280]{0:T(1024)}, u32[]{:S(2)}) copy-start(f32[1280]{0:T(1024)} %param.12) | copy-start | bytes 15364
  53.8 33.6 %collective-permute-start.4 = (bf16[2,2048,256]{2,1,0:T(8,128)(2,1)}, bf16[2,2048,256]{2,1,0:T(8,128)(2,1)}, u32[]{:S(2)}, u32[]{:S(2)}) collective-permute-start(bf16[2,2048,256]{2,1,0:T(8,128)(2,1)} %pad_maximum_fusion.1), channel_id=1, source_target_pairs={{0,4},{1,5},{2,6},{3,7},{4,0},{5,1},{6,2},{7,3},{8,24},{9,25},{10,... | collective-permute-start | bytes 6291464 | tf_op jit(solution)/shard_map/ppermute | solution.py:204
  62.4 25.1 %copy-start.3 = (bf16[2048,256]{1,0:T(8,128)(2,1)S(1)}, bf16[2048,256]{1,0:T(8,128)(2,1)}, u32[]{:S(2)}) copy-start(bf16[2048,256]{1,0:T(8,128)(2,1)} %param.15) | copy-start | bytes 3145732
  65.0 25.9 %all-to-all-start.2 = ((bf16[16,16,1280]{2,1,0:T(8,128)(2,1)}), bf16[16,16,1280]{2,1,0:T(8,128)(2,1)S(1)}, u32[]{:S(2)}, u32[]{:S(2)}) async-start(bf16[16,16,1280]{2,1,0:T(8,128)(2,1)} %bitcast.19), calls=%async_computation.2 | async-start | bytes 1310720 | tf_op jit(solution)/shard_map/all_to_all | solution.py:256
  91.0 28.8 %collective-permute-start.5 = (bf16[4,2048,256]{2,1,0:T(8,128)(2,1)}, bf16[4,2048,256]{2,1,0:T(8,128)(2,1)}, u32[]{:S(2)}, u32[]{:S(2)}) collective-permute-start(bf16[4,2048,256]{2,1,0:T(8,128)(2,1)} %pad_maximum_fusion), channel_id=1, source_target_pairs={{0,8},{1,9},{2,10},{3,11},{4,12},{5,13},{6,14},{7,15},{8,0},{9,1},... | collective-permute-start | bytes 12582920 | tf_op jit(solution)/shard_map/ppermute | solution.py:204
  96.6 16.9 %copy-start.9 = (f32[2048]{0:T(1024)S(1)}, f32[2048]{0:T(1024)}, u32[]{:S(2)}) copy-start(f32[2048]{0:T(1024)} %param.14) | copy-start | bytes 24580
  96.7 9.2 %collective-permute-start.1 = (bf16[128,2048]{1,0:T(8,128)(2,1)S(1)}, bf16[128,2048]{1,0:T(8,128)(2,1)S(1)}, u32[]{:S(2)}, u32[]{:S(2)}) collective-permute-start(bf16[128,2048]{1,0:T(8,128)(2,1)S(1)} %slice.173), channel_id=1, source_target_pairs={{0,16},{1,17},{2,18},{3,19},{4,20},{5,21},{6,22},{7,23},{8,12},{9,... | collective-permute-start | bytes 1572872 | tf_op jit(solution)/shard_map/ppermute | solution.py:204
  106.1 1.0 copy-start.5
  107.1 6.4 %collective-permute-start.2 = (bf16[64,2048]{1,0:T(8,128)(2,1)S(1)}, bf16[64,2048]{1,0:T(8,128)(2,1)S(1)}, u32[]{:S(2)}, u32[]{:S(2)}) collective-permute-start(bf16[64,2048]{1,0:T(8,128)(2,1)S(1)} %slice.174), channel_id=1, source_target_pairs={{0,4},{1,5},{2,6},{3,7},{4,0},{5,1},{6,2},{7,3},{8,24},{9,25},{10,... | collective-permute-start | bytes 786440 | tf_op jit(solution)/shard_map/ppermute | solution.py:204
  119.7 11.4 %copy-start.4 = (bf16[1,512,16,128]{3,2,1,0:T(8,128)(2,1)S(1)}, bf16[1,512,16,128]{3,2,1,0:T(8,128)(2,1)}, u32[]{:S(2)}) copy-start(bf16[1,512,16,128]{3,2,1,0:T(8,128)(2,1)} %param.16) | copy-start | bytes 6291460
  126.8 13.5 %all-to-all-start.3 = ((bf16[4,64,640]{2,1,0:T(8,128)(2,1)}), bf16[4,64,640]{2,1,0:T(8,128)(2,1)S(1)}, u32[]{:S(2)}, u32[]{:S(2)}) async-start(bf16[4,64,640]{2,1,0:T(8,128)(2,1)} %pad_maximum_fusion.3), calls=%async_computation.3 | async-start | bytes 655360 | tf_op jit(solution)/shard_map/all_to_all | solution.py:314
  140.7 4.3 %collective-permute-start.6 = (bf16[64,512]{1,0:T(8,128)(2,1)S(1)}, bf16[64,512]{1,0:T(8,128)(2,1)S(1)}, u32[]{:S(2)}, u32[]{:S(2)}) collective-permute-start(bf16[64,512]{1,0:T(8,128)(2,1)S(1)} %fusion.61), channel_id=1, source_target_pairs={{0,4},{1,5},{2,6},{3,7},{4,0},{5,1},{6,2},{7,3},{8,12},{9,13},{10,... | collective-permute-start | bytes 196616 | tf_op jit(solution)/shard_map/ppermute | solution.py:204
  145.2 5.8 %copy-start.2 = (f32[2,512,512,8]{2,1,3,0:T(8,128)S(1)}, f32[2,512,512,8]{2,1,3,0:T(8,128)}, u32[]{:S(2)}) copy-start(f32[2,512,512,8]{2,1,3,0:T(8,128)} %get-tuple-element.42) | copy-start | bytes 50331652
  151.0 4.0 %copy-start.6 = (bf16[1,512,1,2,128]{4,3,2,1,0:T(2,128)(2,1)S(1)}, bf16[1,512,1,2,128]{4,3,2,1,0:T(2,128)(2,1)}, u32[]{:S(2)}) copy-start(bf16[1,512,1,2,128]{4,3,2,1,0:T(2,128)(2,1)} %get-tuple-element.16) | copy-start | bytes 786436
  155.0 11.0 %copy-start.1 = (bf16[1280,1280]{1,0:T(8,128)(2,1)S(1)}, bf16[1280,1280]{1,0:T(8,128)(2,1)}, u32[]{:S(2)}) copy-start(bf16[1280,1280]{1,0:T(8,128)(2,1)} %param.11) | copy-start | bytes 9830404

commit v2 on v0

--- a/solution.py
+++ b/solution.py
@@ -1,6 +1,11 @@
+import math
+
 import jax
 import jax.numpy as jnp
 from jax import lax
+from jax.experimental import pallas as pl
+from jax.experimental.pallas import tpu as pltpu
+from jax.sharding import Mesh
 from jax.sharding import PartitionSpec as P
 
 VIT_D = 1280
@@ -13,6 +18,7 @@
 
 
 masked_score = -1e30
+LOG2E = math.log2(math.e)
 
 
 def fold_block(running, scores, usable, value_block, forms):
@@ -165,18 +171,474 @@
     return result.reshape(span_rows, kv_local * groups, HD).astype(jnp.bfloat16)[None]
 
 
+def whole(*arrays):
+    return [pl.BlockSpec(memory_space=pltpu.SMEM if a.dtype == jnp.int32 else pltpu.VMEM) for a in arrays]
+
+
+def call(body, outs, *arrays, scratch=(), cost=None):
+    many = isinstance(outs, (tuple, list))
+    return pl.pallas_call(
+        body,
+        out_shape=outs,
+        in_specs=whole(*arrays),
+        out_specs=jax.tree.map(lambda _: pl.BlockSpec(memory_space=pltpu.VMEM), outs),
+        scratch_shapes=list(scratch),
+        cost_estimate=cost,
+    )(*arrays)
+
+
+def pack_heads(rows, owners):
+    patches, kinds, width = rows.shape
+    share = width // owners
+
+    def body(rows_ref, out_ref):
+        for kind in range(kinds):
+            values = rows_ref[:, kind, :]
+            for owner in range(owners):
+                out_ref[owner, :, kind * share : (kind + 1) * share] = values[
+                    :, owner * share : (owner + 1) * share
+                ]
+
+    return call(body, jax.ShapeDtypeStruct((owners, patches, kinds * share), rows.dtype), rows)
+
+
+def vision_attention(spread, patch_counts):
+    owners, patches, width = spread.shape
+    share = width // 3
+    heads = share // VIT_HDIM
+    slots = owners * patches
+    block = 128
+    lanes = 128
+    tail = share - lanes
+    folds = lanes // tail
+    tail_rows = patches // folds
+    factor = VIT_HDIM ** (-0.5) * LOG2E
+
+    def body(count_ref, spread_ref, out_ref):
+        values = spread_ref[...].reshape(slots, width)
+        keys = values[:, share : 2 * share]
+        last = values[:, 2 * share :]
+        usable = lax.broadcasted_iota(jnp.int32, (1, slots), 1) < count_ref[0]
+        lane_head = lax.broadcasted_iota(jnp.int32, (1, share), 1) // VIT_HDIM
+        for start in range(0, slots, block):
+            query = values[start : start + block, :share]
+            result = jnp.zeros((block, share), jnp.float32)
+            for head in range(heads):
+                own = lane_head == head
+                picked = jnp.where(own, query, jnp.zeros_like(query))
+                scores = lax.dot_general(
+                    picked, keys, (((1,), (1,)), ((), ())), preferred_element_type=jnp.float32
+                )
+                scores = jnp.where(usable, scores, masked_score)
+                peak = jnp.max(scores, axis=-1, keepdims=True)
+                weights = jnp.exp2((scores - peak) * factor)
+                weight_sum = jnp.sum(weights, axis=-1, keepdims=True)
+                blended = jnp.dot(
+                    weights.astype(jnp.bfloat16), last, preferred_element_type=jnp.float32
+                )
+                result = jnp.where(own, blended / weight_sum, result)
+            for part in range(block // patches):
+                piece = result[part * patches : (part + 1) * patches]
+                owner = start // patches + part
+                out_ref[owner, :patches, :] = piece[:, :lanes].astype(jnp.bfloat16)
+                out_ref[owner, patches:, :] = jnp.concatenate(
+                    [piece[k * tail_rows : (k + 1) * tail_rows, lanes:] for k in range(folds)], axis=1
+                ).astype(jnp.bfloat16)
+
+    out = jax.ShapeDtypeStruct((owners, patches + tail_rows, lanes), jnp.bfloat16)
+    return call(body, out, patch_counts, spread)
+
+
+def project_norm(places, returned, out_weight, gain, plane, seqs, tps, rows_local):
+    owners, packed_rows, lanes = returned.shape
+    width = out_weight.shape[0]
+    share = width // owners
+    tail = share - lanes
+    folds = lanes // tail
+    patches = packed_rows * folds // (folds + 1)
+    tail_rows = packed_rows - patches
+    token_rows = patches // 4
+    tiles = width // lanes
+
+    def body(places_ref, returned_ref, weight_ref, gain_ref, out_ref, rows_ref):
+        pieces = []
+        for owner in range(owners):
+            pieces.append(returned_ref[owner, :patches, :].astype(jnp.float32))
+            rest = returned_ref[owner, patches:, :].astype(jnp.float32)
+            pieces.append(
+                jnp.concatenate([rest[:, k * tail : (k + 1) * tail] for k in range(folds)], axis=0)
+            )
+        attended = jnp.concatenate(pieces, axis=1).astype(jnp.bfloat16)
+        hidden = jnp.dot(attended, weight_ref[...], preferred_element_type=jnp.float32)
+        ids = lax.broadcasted_iota(jnp.int32, (patches, 1), 0) + places_ref[1]
+        hidden = jnp.where(ids < places_ref[0], hidden, 0.0)
+        centred = hidden - jnp.mean(hidden, axis=-1, keepdims=True)
+        spread_sq = jnp.mean(centred * centred, axis=-1, keepdims=True)
+        normed = centred * lax.rsqrt(spread_sq + 1e-06) * gain_ref[...]
+        for tile in range(tiles):
+            rows_ref[tile] = normed[:, tile * lanes : (tile + 1) * lanes]
+        even = places_ref[2] == 0
+        for xq in range(plane):
+            pair = [
+                jnp.concatenate(
+                    [
+                        rows_ref[tile, pl.ds(2 * xq + core, token_rows, stride=4), :]
+                        for tile in range(tiles)
+                    ],
+                    axis=1,
+                ).astype(jnp.bfloat16)
+                for core in range(2)
+            ]
+            first = jnp.where(even, pair[0], pair[1])
+            second = jnp.where(even, pair[1], pair[0])
+            for sq in range(seqs):
+                for tq in range(tps):
+                    place = (xq * seqs + sq) * tps + tq
+                    cut = slice(sq * rows_local, (sq + 1) * rows_local)
+                    out_ref[place, :, :rows_local] = first[:, cut]
+                    out_ref[place, :, rows_local:] = second[:, cut]
+
+    out = jax.ShapeDtypeStruct((plane * seqs * tps, token_rows, 2 * rows_local), jnp.bfloat16)
+    return call(
+        body, out, places, returned, out_weight, gain[None],
+        scratch=[pltpu.VMEM((tiles, patches, lanes), jnp.float32)],
+    )
+
+
+def merge_partial(order, tokens, own_weight, other_weight):
+    quarters, half, depth = tokens.shape
+    rows_local, columns = own_weight.shape
+    block = 512
+
+    def body(order_ref, tokens_ref, own_ref, other_ref, sent_ref, kept_ref):
+        rows = jnp.concatenate([tokens_ref[order_ref[k]] for k in range(quarters)], axis=0)
+        result = jnp.dot(rows[:, :rows_local], own_ref[...], preferred_element_type=jnp.float32)
+        result = result + jnp.dot(
+            rows[:, rows_local:], other_ref[...], preferred_element_type=jnp.float32
+        )
+        sent_ref[...] = result[: 2 * half].astype(jnp.bfloat16)
+        kept_ref[...] = result[2 * half :]
+
+    weight_spec = pl.BlockSpec((rows_local, block), lambda n: (0, n))
+    out_spec = pl.BlockSpec((2 * half, block), lambda n: (0, n))
+    return pl.pallas_call(
+        body,
+        grid=(columns // block,),
+        out_shape=(
+            jax.ShapeDtypeStruct((2 * half, columns), jnp.bfloat16),
+            jax.ShapeDtypeStruct((2 * half, columns), jnp.float32),
+        ),
+        in_specs=[
+            pl.BlockSpec(memory_space=pltpu.SMEM),
+            pl.BlockSpec((quarters, half, depth), lambda n: (0, 0, 0)),
+            weight_spec,
+            weight_spec,
+        ],
+        out_specs=(out_spec, out_spec),
+    )(order, tokens, own_weight, other_weight)
+
+
+def project_visual(places, kept, received, gain, blocks, tps):
+    half, depth = kept.shape
+    width = blocks[0].shape[1]
+    count = len(blocks)
+    extra = 16
+
+    def body(places_ref, kept_ref, received_ref, gain_ref, *refs):
+        block_refs, out_ref = refs[:count], refs[count]
+        buffers, sems = refs[count + 1 :]
+        copies = [
+            pltpu.make_async_copy(block_refs[k], buffers.at[k], sems.at[k]) for k in range(count)
+        ]
+        for copy in copies:
+            copy.start()
+        embedded = kept_ref[...] + received_ref[...].astype(jnp.float32)
+        squares = jnp.sum(embedded * embedded, axis=-1, keepdims=True)
+        gained = (embedded * gain_ref[...]).astype(jnp.bfloat16)
+        flat = jnp.broadcast_to(squares, (half, 128)).T[:extra]
+        coarse = flat.astype(jnp.bfloat16).astype(jnp.float32)
+        upper = lax.broadcasted_iota(jnp.int32, (extra, half), 0) < extra // 2
+        both = jnp.where(upper, coarse, flat - coarse)
+        both = jnp.concatenate([both, jnp.zeros((extra, width - half), jnp.float32)], axis=1)
+        both = both.astype(jnp.bfloat16)
+        for dest in range(tps):
+            out_ref[dest, 2 * half :, :] = both
+        for k in range(count):
+            copies[k].wait()
+            term = jnp.dot(gained, buffers[k], preferred_element_type=jnp.float32)
+            row = pl.multiple_of(places_ref[2 * k + 1] * half, half)
+            out_ref[places_ref[2 * k], pl.ds(row, half), :] = term.astype(jnp.bfloat16)
+
+    out = jax.ShapeDtypeStruct((tps, 2 * half + extra, width), jnp.bfloat16)
+    return pl.pallas_call(
+        body,
+        out_shape=out,
+        in_specs=[pl.BlockSpec(memory_space=pltpu.SMEM)]
+        + [pl.BlockSpec(memory_space=pltpu.VMEM)] * 3
+        + [pl.BlockSpec(memory_space=pl.ANY)] * count,
+        out_specs=pl.BlockSpec(memory_space=pltpu.VMEM),
+        scratch_shapes=[
+            pltpu.VMEM((count, depth, width), jnp.bfloat16),
+            pltpu.SemaphoreType.DMA((count,)),
+        ],
+    )(places, kept, received, gain[None], *blocks)
+
+
+def finish_visual(sums, half):
+    width = sums.shape[2]
+
+    def body(sums_ref, out_ref):
+        total = jnp.sum(sums_ref[...].astype(jnp.float32), axis=0)
+        flat = total[2 * half : 2 * half + 8] + total[2 * half + 8 :]
+        squares = jnp.broadcast_to(flat[:1, :128], (128, 128)).T[:half, :1]
+        scale = lax.rsqrt(squares / D + 1e-06)
+        out_ref[:half] = (total[:half] * scale).astype(jnp.bfloat16)
+        out_ref[half:] = (total[half : 2 * half] * scale).astype(jnp.bfloat16)
+
+    return call(body, jax.ShapeDtypeStruct((2 * half, width), jnp.bfloat16), sums)
+
+
+def split_queries(block, kv_local):
+    tokens, heads, width = block.shape
+    groups = heads // kv_local
+    wide = block.astype(jnp.float32).reshape(tokens, kv_local, groups, width)
+    return [
+        wide[:, k].reshape(tokens * groups, width).astype(jnp.bfloat16) for k in range(kv_local)
+    ]
+
+
+def prompt_own(queries, span_kv, kv_head):
+    tokens, heads, width = queries.shape
+    kv_local = span_kv.shape[2]
+    groups = heads // kv_local
+    block = 128
+    rows = block * groups
+    factor = HD ** (-0.5) * LOG2E
+
+    def body(queries_ref, span_ref, out_ref, stats_ref):
+        for index in range(tokens // block):
+            start = index * block
+            query = split_queries(queries_ref[start : start + block], kv_local)[kv_head]
+            extent = start + block
+            keys = span_ref[:extent, 0, kv_head, :]
+            values = span_ref[:extent, 1, kv_head, :]
+            scores = lax.dot_general(
+                keys, query, (((1,), (1,)), ((), ())), preferred_element_type=jnp.float32
+            )
+            key_ids = lax.broadcasted_iota(jnp.int32, (extent, rows), 0)
+            token_ids = start + lax.broadcasted_iota(jnp.int32, (extent, rows), 1) // groups
+            scores = jnp.where(key_ids <= token_ids, scores, masked_score)
+            peak = jnp.max(scores, axis=0, keepdims=True)
+            weights = jnp.exp2((scores - peak) * factor)
+            cut = slice(start * groups, extent * groups)
+            stats_ref[0:1, cut] = peak
+            stats_ref[1:2, cut] = jnp.sum(weights, axis=0, keepdims=True)
+            out_ref[:, cut] = lax.dot_general(
+                values, weights.astype(jnp.bfloat16), (((0,), (0,)), ((), ())),
+                preferred_element_type=jnp.float32,
+            )
+
+    outs = (
+        jax.ShapeDtypeStruct((width, tokens * groups), jnp.float32),
+        jax.ShapeDtypeStruct((2, tokens * groups), jnp.float32),
+    )
+    return call(body, outs, queries, span_kv)
+
+
+def prompt_visual(places, queries, own, twin, near, half):
+    tokens, heads, width = queries.shape
+    kv_local = len(near)
+    groups = heads // kv_local
+    block = 128
+    rows = block * groups
+    factor = HD ** (-0.5) * LOG2E
+
+    def body(places_ref, queries_ref, own_ref, twin_ref, *refs):
+        near_refs, out_ref = refs[:-1], refs[-1]
+        split = split_queries(queries_ref[...], kv_local)
+        ids = lax.broadcasted_iota(jnp.int32, (2 * half, 1), 0)
+        ids = jnp.where(ids < half, ids + places_ref[1], ids - half + places_ref[2])
+        seen = ids < places_ref[0]
+        results = []
+        for k in range(kv_local):
+            cut = slice(k * width, (k + 1) * width)
+            keys = jnp.concatenate([own_ref[:half, cut], twin_ref[:half, cut]], axis=0)
+            values = jnp.concatenate([own_ref[half:, cut], twin_ref[half:, cut]], axis=0)
+            scores = lax.dot_general(
+                keys, split[k], (((1,), (1,)), ((), ())), preferred_element_type=jnp.float32
+            )
+            scores = jnp.where(seen, scores, masked_score)
+            stats = near_refs[2 * k + 1][...]
+            peak = jnp.maximum(stats[0:1], jnp.max(scores, axis=0, keepdims=True))
+            weights = jnp.exp2((scores - peak) * factor)
+            decay = jnp.exp2((stats[0:1] - peak) * factor)
+            total = stats[1:2] * decay + jnp.sum(weights, axis=0, keepdims=True)
+            blended = lax.dot_general(
+                values, weights.astype(jnp.bfloat16), (((0,), (0,)), ((), ())),
+                preferred_element_type=jnp.float32,
+            )
+            blended = (blended + near_refs[2 * k][...] * decay) / total
+            results.append(blended.T.reshape(block, 1, groups, width))
+        joined = jnp.concatenate(results, axis=1).reshape(block, heads, width)
+        out_ref[...] = joined.astype(jnp.bfloat16)
+
+    query_spec = pl.BlockSpec((block, heads, width), lambda n: (n, 0, 0))
+    fixed = pl.BlockSpec((2 * half, kv_local * width), lambda n: (0, 0))
+    near_specs = [
+        pl.BlockSpec((width, rows), lambda n: (0, n)),
+        pl.BlockSpec((2, rows), lambda n: (0, n)),
+    ] * kv_local
+    return pl.pallas_call(
+        body,
+        grid=(tokens // block,),
+        out_shape=jax.ShapeDtypeStruct(queries.shape, jnp.bfloat16),
+        in_specs=[pl.BlockSpec(memory_space=pltpu.SMEM), query_spec, fixed, fixed] + near_specs,
+        out_specs=query_spec,
+    )(places, queries, own, twin, *[part for pair in near for part in pair])
+
+
+def swap_pairs(plane, seqs, tps, move):
+    pairs = []
+    for x in range(plane):
+        for c in range(2):
+            for s in range(seqs):
+                for t in range(tps):
+                    x2, c2, s2 = move(x, c, s)
+                    pairs.append((((x * 2 + c) * seqs + s) * tps + t, ((x2 * 2 + c2) * seqs + s2) * tps + t))
+    return pairs
+
+
+def fast_local(
+    vit_qkv,
+    patch_counts,
+    vit_out_weight,
+    vit_norm_gain,
+    merger_weight,
+    lm_norm_gain,
+    kv_weight,
+    queries,
+    span_kv,
+):
+    everything = ("x", "c", "seq", "tp")
+    plane = lax.axis_size("x")
+    seqs = lax.axis_size("seq")
+    tps = lax.axis_size("tp")
+    x, c, s, t = (lax.axis_index(name) for name in everything)
+    owners = seqs * tps
+    patch_rows = vit_qkv.shape[1]
+    token_rows = patch_rows // 4
+    half = tps * token_rows
+    rows_local = merger_weight.shape[0]
+    patch_total = patch_counts[0]
+
+    def swap(value, move):
+        return lax.ppermute(value, everything, swap_pairs(plane, seqs, tps, move))
+
+    def exchange(value, names):
+        return lax.all_to_all(value, names, split_axis=0, concat_axis=0, tiled=True)
+
+    def other_core(x, c, s):
+        return x, 1 - c, s
+
+    def first_hop(x, c, s):
+        return (1 - x, c, s) if c == 0 else (x, c, 1 - s)
+
+    def second_hop(x, c, s):
+        return (x, c, 1 - s) if c == 0 else (1 - x, c, s)
+
+    def other_seq(x, c, s):
+        return x, c, 1 - s
+
+    spread = exchange(pack_heads(vit_qkv[0], owners), ("seq", "tp"))
+    other_rows = swap(merger_weight, other_core)
+
+    near_block = swap(kv_weight, first_hop)
+    side_block = swap(kv_weight, second_hop)
+    far_block = swap(near_block, second_hop)
+    chip_blocks = [kv_weight, near_block, side_block, far_block]
+    kv_blocks = chip_blocks + [swap(block, other_core) for block in chip_blocks]
+
+    near = [prompt_own(queries[0], span_kv[0], k) for k in range(span_kv.shape[3])]
+
+    returned = exchange(vision_attention(spread, patch_counts), ("seq", "tp"))
+    places = jnp.stack([patch_total, (s * tps + t) * patch_rows, c]).astype(jnp.int32)
+    merged = project_norm(
+        places, returned, vit_out_weight, vit_norm_gain, plane, seqs, tps, rows_local
+    )
+
+    tokens = exchange(merged, ("x", "seq", "tp")).reshape(plane * seqs, half, 2 * rows_local)
+
+    def quarter(xq, sq):
+        return xq * seqs + sq
+
+    between = jnp.where(
+        c == 0,
+        jnp.stack([quarter(1 - x, s), quarter(x, 1 - s)]),
+        jnp.stack([quarter(x, 1 - s), quarter(1 - x, s)]),
+    )
+    order = jnp.stack([quarter(1 - x, 1 - s), between[0], between[1], quarter(x, s)])
+    sent, kept = merge_partial(order.astype(jnp.int32), tokens, merger_weight, other_rows)
+    kept = kept + swap(sent, first_hop).astype(jnp.float32)
+    received = swap(kept[:half].astype(jnp.bfloat16), second_hop)
+
+    block_places = []
+    for core_step in range(2):
+        owner = c ^ core_step
+        for far_step in range(2):
+            for hop_step in range(2):
+                kind = x ^ jnp.where(owner == 0, hop_step, far_step)
+                owner_seq = s ^ jnp.where(owner == 0, far_step, hop_step)
+                block_places += [owner * seqs + owner_seq, kind]
+    payload = project_visual(
+        jnp.stack(block_places).astype(jnp.int32), kept[half:], received, lm_norm_gain, kv_blocks, tps
+    )
+    visual = finish_visual(exchange(payload, "tp"), half)
+    twin = swap(visual, other_seq)
+
+    places = jnp.stack([patch_total // 4, s * half, (1 - s) * half]).astype(jnp.int32)
+    return prompt_visual(places, queries[0], visual, twin, near, half)[None]
+
+
 def solution(mesh):
+    sizes = dict(mesh.shape)
+    images, seqs, tps = (sizes[name] for name in ("img", "seq", "tp"))
+    suited = (
+        images == 4
+        and seqs == 2
+        and images * seqs == 2 * tps
+        and VIT_HEADS % (seqs * tps) == 0
+        and KVH % tps == 0
+    )
+    if not suited:
+        placed = (
+            P("img", ("seq", "tp"), None, None),
+            P("img"),
+            P(),
+            P(),
+            P(("img", "seq"), "tp"),
+            P("tp"),
+            P("tp", ("img", "seq")),
+            P("img", "seq", "tp", None),
+            P("img", "seq", None, "tp", None),
+        )
+        return jax.shard_map(
+            local, mesh=mesh, in_specs=placed, out_specs=P("img", "seq", "tp", None), check_vma=False
+        )
+    split = Mesh(
+        mesh.devices.reshape(images // 2, 2, seqs, tps), ("x", "c", "seq", "tp")
+    )
+    image = ("x", "c")
     placed = (
-        P("img", ("seq", "tp"), None, None),
-        P("img"),
+        P(image, ("seq", "tp"), None, None),
+        P(image),
         P(),
         P(),
-        P(("img", "seq"), "tp"),
+        P(("x", "c", "seq"), "tp"),
         P("tp"),
-        P("tp", ("img", "seq")),
-        P("img", "seq", "tp", None),
-        P("img", "seq", None, "tp", None),
+        P("tp", ("x", "c", "seq")),
+        P(image, "seq", "tp", None),
+        P(image, "seq", None, "tp", None),
     )
     return jax.shard_map(
-        local, mesh=mesh, in_specs=placed, out_specs=P("img", "seq", "tp", None), check_vma=False
-    )
+        fast_local, mesh=split, in_specs=placed, out_specs=P(image, "seq", "tp", None), check_vma=False
+    )

time: 270 us -> 140 us (0.52)
  blocking collectives: 67.6 us -> 0 us
  matrix products: 58.1 us -> 0 us
  Pallas kernels: 0 us -> 46.4 us
  local copies, waits for them, and re-layouts: 45.6 us -> 10.3 us
  other arithmetic: 23.2 us -> 3.23 us
  starting transfers between devices: 8.49 us -> 26.4 us
  between operations: 14.7 us -> 0.76 us
    all_gather x5 -> x0, blocking collectives: 59.1 us -> none  [the longest x1 17.9 us: local(): key_piece = lax.all_gather(spread[:, 1], 'tp', axis=0, tiled=True)]
    dot_general x17 -> x0, matrix products: 58.1 us -> none  [the longest x7 26.7 us: fold_block(): jnp.einsum(forms, weights.astype(jnp.bfloat16), value_block, preferred_el...]
    pallas_call x0 -> x9, Pallas kernels: none -> 46.4 us  [the longest x6 27.4 us: call(): pl.pallas_call(body, out_shape=outs, in_specs=whole(*arrays), out_specs=j...]
    all_to_all x2 -> x4, waiting for transfers between devices: 9.24 us -> 35.1 us  [exchange(): return lax.all_to_all(value, names, split_axis=0, concat_axis=0, tiled=True)]
    unnamed x4 -> x0, waiting for transfers between devices: 25.4 us -> none
    ppermute x0 -> x11, waiting for transfers between devices: none -> 17.2 us  [swap(): return lax.ppermute(value, everything, swap_pairs(plane, seqs, tps, move))]
    all_gather x2 -> x0, waiting for transfers between devices: 15.8 us -> none  [the longest x1 15.8 us: local(): lax.all_gather(kv_weight, ('img', 'seq'), axis=1, tiled=True)]
    all_to_all x2 -> x4, starting transfers between devices: 8.41 us -> 19 us  [exchange(): return lax.all_to_all(value, names, split_axis=0, concat_axis=0, tiled=True)]
  transfers between devices with their start and end apart: 5 -> 15, of which waited for: 4 -> 6; matrix products, arithmetic and copies ran while one was open for 35% -> 6% of each run, Pallas kernels for 0% -> 22%
where the time goes in v2:
time: 140 us; the launch traced here: 139 us
  waiting for transfers between devices  52.3 us (37%)
  Pallas kernels  46.4 us (33%)
  starting transfers between devices  26.4 us (19%)
  local copies, waits for them, and re-layouts  10.3 us (7%)
  other arithmetic  3.23 us (2%)
    all_to_all x4, waiting for transfers between devices, exchange(): return lax.all_to_all(value, names, split_axis=0, concat_axis=0, tiled=True)  35.1 us
    pallas_call x6, Pallas kernels, call(): pl.pallas_call(body, out_shape=outs, in_specs=whole(*arrays), out_specs=j...  27.4 us
    all_to_all x4, starting transfers between devices, exchange(): return lax.all_to_all(value, names, split_axis=0, concat_axis=0, tiled=True)  19 us
    ppermute x11, waiting for transfers between devices, swap(): return lax.ppermute(value, everything, swap_pairs(plane, seqs, tps, move))  17.2 us
    unnamed x21, local copies, waits for them, and re-layouts  7.48 us
    ppermute x11, starting transfers between devices, swap(): return lax.ppermute(value, everything, swap_pairs(plane, seqs, tps, move))  7.44 us
    pallas_call x1, Pallas kernels, prompt_visual(): pl.pallas_call(body, grid=(tokens // block,), out_shape=jax.ShapeDtypeStr...  6.94 us
    pallas_call x1, Pallas kernels, project_visual(): pl.pallas_call(body, out_shape=out, in_specs=[pl.BlockSpec(memory_space=p...  6.52 us
  transfers between devices with their start and end apart: 15, of which 6 were waited for; matrix products, arithmetic and copies ran while one was open for 6% of the time, Pallas kernels for 22%

profile of v2, /device:TPU:0, one launch (start us, length us, event | category | flops | bytes accessed | tf_op | source)
XLA Modules:
  0.0 139.4 jit_solution(10240720985005890706)
XLA Ops:
  0.5 2.3 %copy.12 = bf16[1,64,3,1280]{3,2,1,0:T(4,128)(2,1)} copy(bf16[1,64,3,1280]{3,1,2,0:T(8,128)(2,1)} %param.9) | data formatting | bytes 983040 | tf_op args[0]
  2.8 4.5 %shard_map.91 = bf16[8,64,480]{2,1,0:T(8,128)(2,1)} custom-call(bf16[64,3,1280]{2,1,0:T(4,128)(2,1)} %bitcast.40), custom_call_target="tpu_custom_call" | custom-call | tf_op jit(solution)/shard_map/pallas_call | solution.py:180
  7.3 6.8 %all-to-all-start = ((bf16[8,64,480]{2,1,0:T(8,128)(2,1)}), bf16[8,64,480]{2,1,0:T(8,128)(2,1)S(1)}, u32[]{:S(2)}, u32[]{:S(2)}) async-start(bf16[8,64,480]{2,1,0:T(8,128)(2,1)} %shard_map.91), calls=%async_computation | async-start | bytes 1048576 | tf_op jit(solution)/shard_map/all_to_all | solution.py:538
  14.1 1.5 %collective-permute-start.3 = (bf16[2048,256]{1,0:T(8,128)(2,1)}, bf16[2048,256]{1,0:T(8,128)(2,1)}, u32[]{:S(2)}, u32[]{:S(2)}) collective-permute-start(bf16[2048,256]{1,0:T(8,128)(2,1)} %refs_0_.1), channel_id=1, source_target_pairs={{0,16},{1,17},{2,18},{3,19},{4,20},{5,21},{6,22},{7,23},{8,12},{9,... | collective-permute-start | bytes 3145736 | tf_op jit(solution)/shard_map/ppermute | solution.py:535
  16.2 13.9 %all-to-all-done.spread_ref = bf16[8,64,480]{2,1,0:T(8,128)(2,1)S(1)} async-done(((bf16[8,64,480]{2,1,0:T(8,128)(2,1)}), bf16[8,64,480]{2,1,0:T(8,128)(2,1)S(1)}, u32[]{:S(2)}, u32[]{:S(2)}) %all-to-all-start) | async-done | bytes 491552 | tf_op jit(solution)/shard_map/all_to_all | solution.py:538
  30.9 4.6 %shard_map.92 = bf16[8,80,128]{2,1,0:T(8,128)(2,1)} custom-call(s32[1]{0:T(128)} %copy.13.count_ref, bf16[8,64,480]{2,1,0:T(8,128)(2,1)} %copy-done.2), custom_call_target="tpu_custom_call" | custom-call | tf_op jit(solution)/shard_map/pallas_call | solution.py:180
  35.6 3.4 %all-to-all-start.1 = ((bf16[8,80,128]{2,1,0:T(8,128)(2,1)}), bf16[8,80,128]{2,1,0:T(8,128)(2,1)S(1)}, u32[]{:S(2)}, u32[]{:S(2)}) async-start(bf16[8,80,128]{2,1,0:T(8,128)(2,1)} %shard_map.92), calls=%async_computation.1 | async-start | bytes 327680 | tf_op jit(solution)/shard_map/all_to_all | solution.py:538
  40.2 6.5 %all-to-all-done.1.returned_ref = bf16[8,80,128]{2,1,0:T(8,128)(2,1)S(1)} async-done(((bf16[8,80,128]{2,1,0:T(8,128)(2,1)}), bf16[8,80,128]{2,1,0:T(8,128)(2,1)S(1)}, u32[]{:S(2)}, u32[]{:S(2)}) %all-to-all-start.1) | async-done | bytes 163872 | tf_op jit(solution)/shard_map/all_to_all | solution.py:538
  47.3 3.8 %shard_map.93 = bf16[16,16,1280]{2,1,0:T(8,128)(2,1)} custom-call(s32[3]{0:T(128)} %pad_add_fusion.2.places_ref, bf16[8,80,128]{2,1,0:T(8,128)(2,1)} %copy-done.6, bf16[1280,1280]{1,0:T(8,128)(2,1)} %weight_ref.1, f32[1,1280]{1,0:T(1,128)} %broadcast_in_dim.9.gain_ref), custom_call_target="tpu_custom_call" | custom-call | tf_op jit(solution)/shard_map/pallas_call | solution.py:180
  51.2 3.6 %all-to-all-start.2 = ((bf16[16,16,1280]{2,1,0:T(8,128)(2,1)}), bf16[16,16,1280]{2,1,0:T(8,128)(2,1)S(1)}, u32[]{:S(2)}, u32[]{:S(2)}) async-start(bf16[16,16,1280]{2,1,0:T(8,128)(2,1)} %shard_map.93), calls=%async_computation.2 | async-start | bytes 1310720 | tf_op jit(solution)/shard_map/all_to_all | solution.py:538
  54.8 1.8 %collective-permute-start.4 = (bf16[2048,256]{1,0:T(8,128)(2,1)}, bf16[2048,256]{1,0:T(8,128)(2,1)}, u32[]{:S(2)}, u32[]{:S(2)}) collective-permute-start(bf16[2048,256]{1,0:T(8,128)(2,1)} %refs_0_.1), channel_id=1, source_target_pairs={{0,4},{1,5},{2,6},{3,7},{4,0},{5,1},{6,2},{7,3},{8,24},{9,25},{10,... | collective-permute-start | bytes 3145736 | tf_op jit(solution)/shard_map/ppermute | solution.py:535
  57.6 14.7 %all-to-all-done.2 = bf16[16,16,1280]{2,1,0:T(8,128)(2,1)S(1)} async-done(((bf16[16,16,1280]{2,1,0:T(8,128)(2,1)}), bf16[16,16,1280]{2,1,0:T(8,128)(2,1)S(1)}, u32[]{:S(2)}, u32[]{:S(2)}) %all-to-all-start.2) | async-done | bytes 655392 | tf_op jit(solution)/shard_map/all_to_all | solution.py:538
  74.0 5.5 %shard_map.94 = (bf16[128,2048]{1,0:T(8,128)(2,1)}, f32[128,2048]{1,0:T(8,128)}) custom-call(s32[4]{0:T(128)} %pad_add_fusion.1.order_ref, bf16[4,64,1280]{2,1,0:T(8,128)(2,1)} %bitcast.39, bf16[640,2048]{1,0:T(8,128)(2,1)} %own_ref.1, bf16[640,2048]{1,0:T(8,128)(2,1)} %copy-done.1), custom_call_target="tpu_custom_call" | custom-call | tf_op jit(solution)/shard_map/pallas_call | solution.py:324
  80.5 10.6 %collective-permute-done.5.refs_3_ = bf16[2048,256]{1,0:T(8,128)(2,1)} collective-permute-done((bf16[2048,256]{1,0:T(8,128)(2,1)}, bf16[2048,256]{1,0:T(8,128)(2,1)}, u32[]{:S(2)}, u32[]{:S(2)}) %collective-permute-start.5) | collective-permute-done | bytes 1048608 | tf_op jit(solution)/shard_map/ppermute | solution.py:535
  91.1 1.3 convert_add_fusion
  93.2 1.6 %collective-permute-start.2 = (bf16[64,2048]{1,0:T(8,128)(2,1)}, bf16[64,2048]{1,0:T(8,128)(2,1)S(1)}, u32[]{:S(2)}, u32[]{:S(2)}) collective-permute-start(bf16[64,2048]{1,0:T(8,128)(2,1)} %slice.15), channel_id=1, source_target_pairs={{0,4},{1,5},{2,6},{3,7},{4,0},{5,1},{6,2},{7,3},{8,24},{9,25},{10,... | collective-permute-start | bytes 786440 | tf_op jit(solution)/shard_map/ppermute | solution.py:535
  96.3 3.4 %collective-permute-done.2.received_ref = bf16[64,2048]{1,0:T(8,128)(2,1)S(1)} collective-permute-done((bf16[64,2048]{1,0:T(8,128)(2,1)}, bf16[64,2048]{1,0:T(8,128)(2,1)S(1)}, u32[]{:S(2)}, u32[]{:S(2)}) %collective-permute-start.2) | collective-permute-done | bytes 262176 | tf_op jit(solution)/shard_map/ppermute | solution.py:535
  100.4 6.5 %shard_map.95 = bf16[4,144,256]{2,1,0:T(8,128)(2,1)} custom-call(s32[16]{0:T(128)} %stack.109.places_ref, f32[64,2048]{1,0:T(8,128)} %slice.12.kept_ref, bf16[64,2048]{1,0:T(8,128)(2,1)} %copy-done.7, f32[1,2048]{1,0:T(1,128)} %bitcast.43, bf16[2048,256]{1,0:T(8,128)(2,1)} %refs_0_.1, bf16[2048,256]{1,0:T(8,128)(2,1)} %collective-permute-done.3.refs_1_, ...), custom_call_target="tpu_custom_call" | custom-call | tf_op jit(solution)/shard_map/pallas_call | solution.py:373
  107.0 5.2 %all-to-all-start.3 = ((bf16[4,144,256]{2,1,0:T(8,128)(2,1)}), bf16[4,144,256]{2,1,0:T(8,128)(2,1)S(1)}, u32[]{:S(2)}, u32[]{:S(2)}) async-start(bf16[4,144,256]{2,1,0:T(8,128)(2,1)} %shard_map.95), calls=%async_computation.3 | async-start | bytes 589824 | tf_op jit(solution)/shard_map/all_to_all | solution.py:538
  112.2 6.4 %shard_map.97 = (f32[128,4096]{1,0:T(8,128)}, f32[2,4096]{1,0:T(2,128)}) custom-call(bf16[512,16,128]{2,1,0:T(8,128)(2,1)} %bitcast.36, bf16[512,2,2,128]{3,2,1,0:T(2,128)(2,1)} %bitcast.41), custom_call_target="tpu_custom_call" | custom-call | tf_op jit(solution)/shard_map/pallas_call | solution.py:180
  118.6 6.4 %shard_map.98 = (f32[128,4096]{1,0:T(8,128)}, f32[2,4096]{1,0:T(2,128)}) custom-call(bf16[512,16,128]{2,1,0:T(8,128)(2,1)} %bitcast.37, bf16[512,2,2,128]{3,2,1,0:T(2,128)(2,1)} %bitcast.42), custom_call_target="tpu_custom_call" | custom-call | tf_op jit(solution)/shard_map/pallas_call | solution.py:180
  125.6 1.7 %shard_map.96.own_ref = bf16[128,256]{1,0:T(8,128)(2,1)} custom-call(bf16[4,144,256]{2,1,0:T(8,128)(2,1)} %copy-done.3), custom_call_target="tpu_custom_call" | custom-call | tf_op jit(solution)/shard_map/pallas_call | solution.py:180
  128.7 3.2 %collective-permute-done.10.twin_ref = bf16[128,256]{1,0:T(8,128)(2,1)S(1)} collective-permute-done((bf16[128,256]{1,0:T(8,128)(2,1)}, bf16[128,256]{1,0:T(8,128)(2,1)S(1)}, u32[]{:S(2)}, u32[]{:S(2)}) %collective-permute-start.10) | collective-permute-done | bytes 65568 | tf_op jit(solution)/shard_map/ppermute | solution.py:535
  132.5 6.9 %shard_map.99 = bf16[512,16,128]{2,1,0:T(8,128)(2,1)} custom-call(s32[3]{0:T(128)} %pad_add_fusion.places_ref, bf16[512,16,128]{2,1,0:T(8,128)(2,1)} %bitcast.38, bf16[128,256]{1,0:T(8,128)(2,1)} %shard_map.96.own_ref, bf16[128,256]{1,0:T(8,128)(2,1)} %copy-done.8, f32[128,4096]{1,0:T(8,128)} %get-tuple-element.13.refs_0_, ...), custom_call_target="tpu_custom_call" | custom-call | tf_op jit(solution)/shard_map/pallas_call | solution.py:491
  (45 shorter events, 12.5 us)
Async XLA Ops:
  0.0 39.0 %copy-start.9 = (f32[1280]{0:T(1024)S(1)}, f32[1280]{0:T(1024)}, u32[]{:S(2)}) copy-start(f32[1280]{0:T(1024)} %param.12) | copy-start | bytes 15364
  0.0 72.3 %collective-permute-start = (bf16[640,2048]{1,0:T(8,128)(2,1)}, bf16[640,2048]{1,0:T(8,128)(2,1)S(1)}, u32[]{:S(2)}, u32[]{:S(2)}) collective-permute-start(bf16[640,2048]{1,0:T(8,128)(2,1)} %own_ref.1), channel_id=1, source_target_pairs={{0,8},{1,9},{2,10},{3,11},{4,12},{5,13},{6,14},{7,15},{8,0},{9,1},... | collective-permute-start | bytes 7864328 | tf_op jit(solution)/shard_map/ppermute | solution.py:535
  7.3 22.9 %all-to-all-start = ((bf16[8,64,480]{2,1,0:T(8,128)(2,1)}), bf16[8,64,480]{2,1,0:T(8,128)(2,1)S(1)}, u32[]{:S(2)}, u32[]{:S(2)}) async-start(bf16[8,64,480]{2,1,0:T(8,128)(2,1)} %shard_map.91), calls=%async_computation | async-start | bytes 1048576 | tf_op jit(solution)/shard_map/all_to_all | solution.py:538
  14.1 42.5 %collective-permute-start.3 = (bf16[2048,256]{1,0:T(8,128)(2,1)}, bf16[2048,256]{1,0:T(8,128)(2,1)}, u32[]{:S(2)}, u32[]{:S(2)}) collective-permute-start(bf16[2048,256]{1,0:T(8,128)(2,1)} %refs_0_.1), channel_id=1, source_target_pairs={{0,16},{1,17},{2,18},{3,19},{4,20},{5,21},{6,22},{7,23},{8,12},{9,... | collective-permute-start | bytes 3145736 | tf_op jit(solution)/shard_map/ppermute | solution.py:535
  30.1 0.8 copy-start.2
  35.6 11.1 %all-to-all-start.1 = ((bf16[8,80,128]{2,1,0:T(8,128)(2,1)}), bf16[8,80,128]{2,1,0:T(8,128)(2,1)S(1)}, u32[]{:S(2)}, u32[]{:S(2)}) async-start(bf16[8,80,128]{2,1,0:T(8,128)(2,1)} %shard_map.92), calls=%async_computation.1 | async-start | bytes 327680 | tf_op jit(solution)/shard_map/all_to_all | solution.py:538
  46.7 0.7 copy-start.6
  51.2 21.1 %all-to-all-start.2 = ((bf16[16,16,1280]{2,1,0:T(8,128)(2,1)}), bf16[16,16,1280]{2,1,0:T(8,128)(2,1)S(1)}, u32[]{:S(2)}, u32[]{:S(2)}) async-start(bf16[16,16,1280]{2,1,0:T(8,128)(2,1)} %shard_map.93), calls=%async_computation.2 | async-start | bytes 1310720 | tf_op jit(solution)/shard_map/all_to_all | solution.py:538
  54.8 25.7 %collective-permute-start.4 = (bf16[2048,256]{1,0:T(8,128)(2,1)}, bf16[2048,256]{1,0:T(8,128)(2,1)}, u32[]{:S(2)}, u32[]{:S(2)}) collective-permute-start(bf16[2048,256]{1,0:T(8,128)(2,1)} %refs_0_.1), channel_id=1, source_target_pairs={{0,4},{1,5},{2,6},{3,7},{4,0},{5,1},{6,2},{7,3},{8,24},{9,25},{10,... | collective-permute-start | bytes 3145736 | tf_op jit(solution)/shard_map/ppermute | solution.py:535
  56.6 34.5 %collective-permute-start.5 = (bf16[2048,256]{1,0:T(8,128)(2,1)}, bf16[2048,256]{1,0:T(8,128)(2,1)}, u32[]{:S(2)}, u32[]{:S(2)}) collective-permute-start(bf16[2048,256]{1,0:T(8,128)(2,1)} %collective-permute-done.3.refs_1_), channel_id=1, source_target_pairs={{0,4},{1,5},{2,6},{3,7},{4,0},{5,1},{6,2},{7,3},{8,24},{9,25},{10,... | collective-permute-start | bytes 3145736 | tf_op jit(solution)/shard_map/ppermute | solution.py:535
  72.3 0.9 copy-start
  72.3 1.7 %copy-start.1 = (bf16[640,2048]{1,0:T(8,128)(2,1)}, bf16[640,2048]{1,0:T(8,128)(2,1)S(1)}, u32[]{:S(2)}) copy-start(bf16[640,2048]{1,0:T(8,128)(2,1)S(1)} %collective-permute-done.other_ref) | copy-start | bytes 7864324
  79.5 11.6 %collective-permute-start.1 = (bf16[128,2048]{1,0:T(8,128)(2,1)}, bf16[128,2048]{1,0:T(8,128)(2,1)S(1)}, u32[]{:S(2)}, u32[]{:S(2)}) collective-permute-start(bf16[128,2048]{1,0:T(8,128)(2,1)} %get-tuple-element.12), channel_id=1, source_target_pairs={{0,16},{1,17},{2,18},{3,19},{4,20},{5,21},{6,22},{7,23},{8,12},{9,... | collective-permute-start | bytes 1572872 | tf_op jit(solution)/shard_map/ppermute | solution.py:535
  80.0 16.3 %collective-permute-start.6 = (bf16[2048,256]{1,0:T(8,128)(2,1)}, bf16[2048,256]{1,0:T(8,128)(2,1)S(1)}, u32[]{:S(2)}, u32[]{:S(2)}) collective-permute-start(bf16[2048,256]{1,0:T(8,128)(2,1)} %refs_0_.1), channel_id=1, source_target_pairs={{0,8},{1,9},{2,10},{3,11},{4,12},{5,13},{6,14},{7,15},{8,0},{9,1},... | collective-permute-start | bytes 3145736 | tf_op jit(solution)/shard_map/ppermute | solution.py:535
  80.0 16.3 %collective-permute-start.7 = (bf16[2048,256]{1,0:T(8,128)(2,1)}, bf16[2048,256]{1,0:T(8,128)(2,1)S(1)}, u32[]{:S(2)}, u32[]{:S(2)}) collective-permute-start(bf16[2048,256]{1,0:T(8,128)(2,1)} %collective-permute-done.3.refs_1_), channel_id=1, source_target_pairs={{0,8},{1,9},{2,10},{3,11},{4,12},{5,13},{6,14},{7,15},{8,0},{9,1},... | collective-permute-start | bytes 3145736 | tf_op jit(solution)/shard_map/ppermute | solution.py:535
  80.5 15.8 %collective-permute-start.8 = (bf16[2048,256]{1,0:T(8,128)(2,1)}, bf16[2048,256]{1,0:T(8,128)(2,1)}, u32[]{:S(2)}, u32[]{:S(2)}) collective-permute-start(bf16[2048,256]{1,0:T(8,128)(2,1)} %collective-permute-done.4.refs_2_), channel_id=1, source_target_pairs={{0,8},{1,9},{2,10},{3,11},{4,12},{5,13},{6,14},{7,15},{8,0},{9,1},... | collective-permute-start | bytes 3145736 | tf_op jit(solution)/shard_map/ppermute | solution.py:535
  91.1 5.2 %collective-permute-start.9 = (bf16[2048,256]{1,0:T(8,128)(2,1)}, bf16[2048,256]{1,0:T(8,128)(2,1)}, u32[]{:S(2)}, u32[]{:S(2)}) collective-permute-start(bf16[2048,256]{1,0:T(8,128)(2,1)} %collective-permute-done.5.refs_3_), channel_id=1, source_target_pairs={{0,8},{1,9},{2,10},{3,11},{4,12},{5,13},{6,14},{7,15},{8,0},{9,1},... | collective-permute-start | bytes 3145736 | tf_op jit(solution)/shard_map/ppermute | solution.py:535
  93.2 6.6 %collective-permute-start.2 = (bf16[64,2048]{1,0:T(8,128)(2,1)}, bf16[64,2048]{1,0:T(8,128)(2,1)S(1)}, u32[]{:S(2)}, u32[]{:S(2)}) collective-permute-start(bf16[64,2048]{1,0:T(8,128)(2,1)} %slice.15), channel_id=1, source_target_pairs={{0,4},{1,5},{2,6},{3,7},{4,0},{5,1},{6,2},{7,3},{8,24},{9,25},{10,... | collective-permute-start | bytes 786440 | tf_op jit(solution)/shard_map/ppermute | solution.py:535
  96.3 3.5 %copy-start.4 = (bf16[2048,256]{1,0:T(8,128)(2,1)}, bf16[2048,256]{1,0:T(8,128)(2,1)S(1)}, u32[]{:S(2)}) copy-start(bf16[2048,256]{1,0:T(8,128)(2,1)S(1)} %collective-permute-done.6.refs_4_) | copy-start | bytes 3145732
  96.3 3.5 %copy-start.5 = (bf16[2048,256]{1,0:T(8,128)(2,1)}, bf16[2048,256]{1,0:T(8,128)(2,1)S(1)}, u32[]{:S(2)}) copy-start(bf16[2048,256]{1,0:T(8,128)(2,1)S(1)} %collective-permute-done.7.refs_5_) | copy-start | bytes 3145732
  99.7 0.7 copy-start.7
  107.0 17.9 %all-to-all-start.3 = ((bf16[4,144,256]{2,1,0:T(8,128)(2,1)}), bf16[4,144,256]{2,1,0:T(8,128)(2,1)S(1)}, u32[]{:S(2)}, u32[]{:S(2)}) async-start(bf16[4,144,256]{2,1,0:T(8,128)(2,1)} %shard_map.95), calls=%async_computation.3 | async-start | bytes 589824 | tf_op jit(solution)/shard_map/all_to_all | solution.py:538
  124.9 0.7 copy-start.3
  127.4 4.5 %collective-permute-start.10 = (bf16[128,256]{1,0:T(8,128)(2,1)}, bf16[128,256]{1,0:T(8,128)(2,1)S(1)}, u32[]{:S(2)}, u32[]{:S(2)}) collective-permute-start(bf16[128,256]{1,0:T(8,128)(2,1)} %shard_map.96.own_ref), channel_id=1, source_target_pairs={{0,4},{1,5},{2,6},{3,7},{4,0},{5,1},{6,2},{7,3},{8,12},{9,13},{10,... | collective-permute-start | bytes 196616 | tf_op jit(solution)/shard_map/ppermute | solution.py:535
  (1 other events, 0.6 us)

commit v3 on v2

--- a/solution.py
+++ b/solution.py
@@ -175,25 +175,37 @@
     return [pl.BlockSpec(memory_space=pltpu.SMEM if a.dtype == jnp.int32 else pltpu.VMEM) for a in arrays]
 
 
-def call(body, outs, *arrays, scratch=(), cost=None):
-    many = isinstance(outs, (tuple, list))
+def onchip(array):
+    return pltpu.with_memory_space_constraint(array, pltpu.VMEM)
+
+
+def offchip(array):
+    return pltpu.with_memory_space_constraint(array, pltpu.HBM)
+
+
+def grant(mib):
+    return pltpu.CompilerParams(vmem_limit_bytes=mib << 20)
+
+
+def call(body, outs, *arrays, scratch=(), stay=(), mib=12):
+    arrays = [onchip(a) if k in stay else a for k, a in enumerate(arrays)]
     return pl.pallas_call(
         body,
         out_shape=outs,
         in_specs=whole(*arrays),
         out_specs=jax.tree.map(lambda _: pl.BlockSpec(memory_space=pltpu.VMEM), outs),
         scratch_shapes=list(scratch),
-        cost_estimate=cost,
+        compiler_params=grant(mib),
     )(*arrays)
 
 
 def pack_heads(rows, owners):
-    patches, kinds, width = rows.shape
+    kinds, patches, width = rows.shape
     share = width // owners
 
     def body(rows_ref, out_ref):
         for kind in range(kinds):
-            values = rows_ref[:, kind, :]
+            values = rows_ref[kind]
             for owner in range(owners):
                 out_ref[owner, :, kind * share : (kind + 1) * share] = values[
                     :, owner * share : (owner + 1) * share
@@ -202,7 +214,7 @@
     return call(body, jax.ShapeDtypeStruct((owners, patches, kinds * share), rows.dtype), rows)
 
 
-def vision_attention(spread, patch_counts):
+def vision_attention(spread, scalars):
     owners, patches, width = spread.shape
     share = width // 3
     heads = share // VIT_HDIM
@@ -214,11 +226,11 @@
     tail_rows = patches // folds
     factor = VIT_HDIM ** (-0.5) * LOG2E
 
-    def body(count_ref, spread_ref, out_ref):
+    def body(scalars_ref, spread_ref, out_ref):
         values = spread_ref[...].reshape(slots, width)
         keys = values[:, share : 2 * share]
         last = values[:, 2 * share :]
-        usable = lax.broadcasted_iota(jnp.int32, (1, slots), 1) < count_ref[0]
+        usable = lax.broadcasted_iota(jnp.int32, (1, slots), 1) < scalars_ref[0]
         lane_head = lax.broadcasted_iota(jnp.int32, (1, share), 1) // VIT_HDIM
         for start in range(0, slots, block):
             query = values[start : start + block, :share]
@@ -246,21 +258,20 @@
                 ).astype(jnp.bfloat16)
 
     out = jax.ShapeDtypeStruct((owners, patches + tail_rows, lanes), jnp.bfloat16)
-    return call(body, out, patch_counts, spread)
-
-
-def project_norm(places, returned, out_weight, gain, plane, seqs, tps, rows_local):
+    return call(body, out, scalars, spread, stay=(1,))
+
+
+def project_norm(scalars, returned, out_weight, gain, plane, seqs, tps, rows_local):
     owners, packed_rows, lanes = returned.shape
     width = out_weight.shape[0]
     share = width // owners
     tail = share - lanes
     folds = lanes // tail
     patches = packed_rows * folds // (folds + 1)
-    tail_rows = packed_rows - patches
     token_rows = patches // 4
     tiles = width // lanes
 
-    def body(places_ref, returned_ref, weight_ref, gain_ref, out_ref, rows_ref):
+    def body(scalars_ref, returned_ref, weight_ref, gain_ref, out_ref, rows_ref):
         pieces = []
         for owner in range(owners):
             pieces.append(returned_ref[owner, :patches, :].astype(jnp.float32))
@@ -270,14 +281,14 @@
             )
         attended = jnp.concatenate(pieces, axis=1).astype(jnp.bfloat16)
         hidden = jnp.dot(attended, weight_ref[...], preferred_element_type=jnp.float32)
-        ids = lax.broadcasted_iota(jnp.int32, (patches, 1), 0) + places_ref[1]
-        hidden = jnp.where(ids < places_ref[0], hidden, 0.0)
+        ids = lax.broadcasted_iota(jnp.int32, (patches, 1), 0) + scalars_ref[1]
+        hidden = jnp.where(ids < scalars_ref[0], hidden, 0.0)
         centred = hidden - jnp.mean(hidden, axis=-1, keepdims=True)
         spread_sq = jnp.mean(centred * centred, axis=-1, keepdims=True)
         normed = centred * lax.rsqrt(spread_sq + 1e-06) * gain_ref[...]
         for tile in range(tiles):
             rows_ref[tile] = normed[:, tile * lanes : (tile + 1) * lanes]
-        even = places_ref[2] == 0
+        even = scalars_ref[2] == 0
         for xq in range(plane):
             pair = [
                 jnp.concatenate(
@@ -300,18 +311,19 @@
 
     out = jax.ShapeDtypeStruct((plane * seqs * tps, token_rows, 2 * rows_local), jnp.bfloat16)
     return call(
-        body, out, places, returned, out_weight, gain[None],
+        body, out, scalars, returned, out_weight, gain[None],
         scratch=[pltpu.VMEM((tiles, patches, lanes), jnp.float32)],
-    )
-
-
-def merge_partial(order, tokens, own_weight, other_weight):
+        stay=(1,), mib=16,
+    )
+
+
+def merge_partial(scalars, tokens, own_weight, other_weight):
     quarters, half, depth = tokens.shape
     rows_local, columns = own_weight.shape
     block = 512
 
-    def body(order_ref, tokens_ref, own_ref, other_ref, sent_ref, kept_ref):
-        rows = jnp.concatenate([tokens_ref[order_ref[k]] for k in range(quarters)], axis=0)
+    def body(scalars_ref, tokens_ref, own_ref, other_ref, sent_ref, kept_ref):
+        rows = jnp.concatenate([tokens_ref[scalars_ref[3 + k]] for k in range(quarters)], axis=0)
         result = jnp.dot(rows[:, :rows_local], own_ref[...], preferred_element_type=jnp.float32)
         result = result + jnp.dot(
             rows[:, rows_local:], other_ref[...], preferred_element_type=jnp.float32
@@ -335,16 +347,32 @@
             weight_spec,
         ],
         out_specs=(out_spec, out_spec),
-    )(order, tokens, own_weight, other_weight)
-
-
-def project_visual(places, kept, received, gain, blocks, tps):
+        compiler_params=grant(24),
+    )(scalars, onchip(tokens), offchip(own_weight), offchip(other_weight))
+
+
+def add_received(kept, received):
+    half = kept.shape[0] // 2
+
+    def body(kept_ref, received_ref, sent_ref, out_ref):
+        result = kept_ref[...] + received_ref[...].astype(jnp.float32)
+        sent_ref[...] = result[:half].astype(jnp.bfloat16)
+        out_ref[...] = result[half:]
+
+    outs = (
+        jax.ShapeDtypeStruct((half, kept.shape[1]), jnp.bfloat16),
+        jax.ShapeDtypeStruct((half, kept.shape[1]), jnp.float32),
+    )
+    return call(body, outs, kept, received, stay=(0, 1))
+
+
+def project_visual(scalars, kept, received, gain, blocks, tps):
     half, depth = kept.shape
     width = blocks[0].shape[1]
     count = len(blocks)
     extra = 16
 
-    def body(places_ref, kept_ref, received_ref, gain_ref, *refs):
+    def body(scalars_ref, kept_ref, received_ref, gain_ref, *refs):
         block_refs, out_ref = refs[:count], refs[count]
         buffers, sems = refs[count + 1 :]
         copies = [
@@ -366,8 +394,8 @@
         for k in range(count):
             copies[k].wait()
             term = jnp.dot(gained, buffers[k], preferred_element_type=jnp.float32)
-            row = pl.multiple_of(places_ref[2 * k + 1] * half, half)
-            out_ref[places_ref[2 * k], pl.ds(row, half), :] = term.astype(jnp.bfloat16)
+            row = pl.multiple_of(scalars_ref[11 + 2 * k] * half, half)
+            out_ref[scalars_ref[10 + 2 * k], pl.ds(row, half), :] = term.astype(jnp.bfloat16)
 
     out = jax.ShapeDtypeStruct((tps, 2 * half + extra, width), jnp.bfloat16)
     return pl.pallas_call(
@@ -381,7 +409,8 @@
             pltpu.VMEM((count, depth, width), jnp.bfloat16),
             pltpu.SemaphoreType.DMA((count,)),
         ],
-    )(places, kept, received, gain[None], *blocks)
+        compiler_params=grant(24),
+    )(scalars, onchip(kept), onchip(received), gain[None], *[offchip(block) for block in blocks])
 
 
 def finish_visual(sums, half):
@@ -395,7 +424,7 @@
         out_ref[:half] = (total[:half] * scale).astype(jnp.bfloat16)
         out_ref[half:] = (total[half : 2 * half] * scale).astype(jnp.bfloat16)
 
-    return call(body, jax.ShapeDtypeStruct((2 * half, width), jnp.bfloat16), sums)
+    return call(body, jax.ShapeDtypeStruct((2 * half, width), jnp.bfloat16), sums, stay=(0,))
 
 
 def split_queries(block, kv_local):
@@ -416,12 +445,14 @@
     factor = HD ** (-0.5) * LOG2E
 
     def body(queries_ref, span_ref, out_ref, stats_ref):
+        every_key = span_ref[:, 0, kv_head, :]
+        every_value = span_ref[:, 1, kv_head, :]
         for index in range(tokens // block):
             start = index * block
             query = split_queries(queries_ref[start : start + block], kv_local)[kv_head]
             extent = start + block
-            keys = span_ref[:extent, 0, kv_head, :]
-            values = span_ref[:extent, 1, kv_head, :]
+            keys = every_key[:extent]
+            values = every_value[:extent]
             scores = lax.dot_general(
                 keys, query, (((1,), (1,)), ((), ())), preferred_element_type=jnp.float32
             )
@@ -442,10 +473,10 @@
         jax.ShapeDtypeStruct((width, tokens * groups), jnp.float32),
         jax.ShapeDtypeStruct((2, tokens * groups), jnp.float32),
     )
-    return call(body, outs, queries, span_kv)
-
-
-def prompt_visual(places, queries, own, twin, near, half):
+    return call(body, outs, offchip(queries), offchip(span_kv), mib=24)
+
+
+def prompt_visual(scalars, queries, own, twin, near, half):
     tokens, heads, width = queries.shape
     kv_local = len(near)
     groups = heads // kv_local
@@ -453,12 +484,12 @@
     rows = block * groups
     factor = HD ** (-0.5) * LOG2E
 
-    def body(places_ref, queries_ref, own_ref, twin_ref, *refs):
+    def body(scalars_ref, queries_ref, own_ref, twin_ref, *refs):
         near_refs, out_ref = refs[:-1], refs[-1]
         split = split_queries(queries_ref[...], kv_local)
         ids = lax.broadcasted_iota(jnp.int32, (2 * half, 1), 0)
-        ids = jnp.where(ids < half, ids + places_ref[1], ids - half + places_ref[2])
-        seen = ids < places_ref[0]
+        ids = jnp.where(ids < half, ids + scalars_ref[8], ids - half + scalars_ref[9])
+        seen = ids < scalars_ref[7]
         results = []
         for k in range(kv_local):
             cut = slice(k * width, (k + 1) * width)
@@ -494,7 +525,8 @@
         out_shape=jax.ShapeDtypeStruct(queries.shape, jnp.bfloat16),
         in_specs=[pl.BlockSpec(memory_space=pltpu.SMEM), query_spec, fixed, fixed] + near_specs,
         out_specs=query_spec,
-    )(places, queries, own, twin, *[part for pair in near for part in pair])
+        compiler_params=grant(24),
+    )(scalars, offchip(queries), onchip(own), onchip(twin), *[offchip(part) for pair in near for part in pair])
 
 
 def swap_pairs(plane, seqs, tps, move):
@@ -549,54 +581,56 @@
     def other_seq(x, c, s):
         return x, c, 1 - s
 
-    spread = exchange(pack_heads(vit_qkv[0], owners), ("seq", "tp"))
+    def quarter(xq, sq):
+        return xq * seqs + sq
+
+    even = c == 0
+    scalars = [patch_total, (s * tps + t) * patch_rows, c, quarter(1 - x, 1 - s)]
+    scalars.append(jnp.where(even, quarter(1 - x, s), quarter(x, 1 - s)))
+    scalars.append(jnp.where(even, quarter(x, 1 - s), quarter(1 - x, s)))
+    scalars += [quarter(x, s), patch_total // 4, s * half, (1 - s) * half]
+    for core_step in range(2):
+        owner = c ^ core_step
+        for far_step in range(2):
+            for hop_step in range(2):
+                owner_seq = s ^ jnp.where(owner == 0, far_step, hop_step)
+                scalars += [owner * seqs + owner_seq, x ^ jnp.where(owner == 0, hop_step, far_step)]
+    scalars = jnp.stack(scalars).astype(jnp.int32)
+
     other_rows = swap(merger_weight, other_core)
+    packed = pack_heads(jnp.transpose(vit_qkv[0], (1, 0, 2)), owners)
+    spread = exchange(packed, ("seq", "tp"))
 
     near_block = swap(kv_weight, first_hop)
     side_block = swap(kv_weight, second_hop)
     far_block = swap(near_block, second_hop)
     chip_blocks = [kv_weight, near_block, side_block, far_block]
-    kv_blocks = chip_blocks + [swap(block, other_core) for block in chip_blocks]
-
-    near = [prompt_own(queries[0], span_kv[0], k) for k in range(span_kv.shape[3])]
-
-    returned = exchange(vision_attention(spread, patch_counts), ("seq", "tp"))
-    places = jnp.stack([patch_total, (s * tps + t) * patch_rows, c]).astype(jnp.int32)
+    kv_blocks = list(chip_blocks)
+    for block in chip_blocks:
+        kv_blocks.append(swap(block, other_core))
+
+    near = []
+    for k in range(span_kv.shape[3]):
+        near.append(prompt_own(queries[0], span_kv[0], k))
+
+    attended = vision_attention(spread, scalars)
+    returned = exchange(attended, ("seq", "tp"))
     merged = project_norm(
-        places, returned, vit_out_weight, vit_norm_gain, plane, seqs, tps, rows_local
+        scalars, returned, vit_out_weight, vit_norm_gain, plane, seqs, tps, rows_local
     )
 
     tokens = exchange(merged, ("x", "seq", "tp")).reshape(plane * seqs, half, 2 * rows_local)
-
-    def quarter(xq, sq):
-        return xq * seqs + sq
-
-    between = jnp.where(
-        c == 0,
-        jnp.stack([quarter(1 - x, s), quarter(x, 1 - s)]),
-        jnp.stack([quarter(x, 1 - s), quarter(1 - x, s)]),
-    )
-    order = jnp.stack([quarter(1 - x, 1 - s), between[0], between[1], quarter(x, s)])
-    sent, kept = merge_partial(order.astype(jnp.int32), tokens, merger_weight, other_rows)
-    kept = kept + swap(sent, first_hop).astype(jnp.float32)
-    received = swap(kept[:half].astype(jnp.bfloat16), second_hop)
-
-    block_places = []
-    for core_step in range(2):
-        owner = c ^ core_step
-        for far_step in range(2):
-            for hop_step in range(2):
-                kind = x ^ jnp.where(owner == 0, hop_step, far_step)
-                owner_seq = s ^ jnp.where(owner == 0, far_step, hop_step)
-                block_places += [owner * seqs + owner_seq, kind]
-    payload = project_visual(
-        jnp.stack(block_places).astype(jnp.int32), kept[half:], received, lm_norm_gain, kv_blocks, tps
-    )
-    visual = finish_visual(exchange(payload, "tp"), half)
+    sent, kept = merge_partial(scalars, tokens, merger_weight, other_rows)
+    received = swap(sent, first_hop)
+    sent, kept = add_received(kept, received)
+    received = swap(sent, second_hop)
+
+    payload = project_visual(scalars, kept, received, lm_norm_gain, kv_blocks, tps)
+    sums = exchange(payload, "tp")
+    visual = finish_visual(sums, half)
     twin = swap(visual, other_seq)
 
-    places = jnp.stack([patch_total // 4, s * half, (1 - s) * half]).astype(jnp.int32)
-    return prompt_visual(places, queries[0], visual, twin, near, half)[None]
+    return prompt_visual(scalars, queries[0], visual, twin, near, half)[None]
 
 
 def solution(mesh):
@@ -639,6 +673,7 @@
         P(image, "seq", "tp", None),
         P(image, "seq", None, "tp", None),
     )
+
     return jax.shard_map(
         fast_local, mesh=split, in_specs=placed, out_specs=P(image, "seq", "tp", None), check_vma=False
     )

time: 140 us -> 128 us (0.914)
  Pallas kernels: 46.4 us -> 31.4 us
  blocking collectives: 0 us -> 12.1 us
  starting transfers between devices: 26.4 us -> 22.8 us
  other arithmetic: 3.23 us -> 0 us
  local copies, waits for them, and re-layouts: 10.3 us -> 7.53 us
    ppermute x11, waiting for transfers between devices: 17.2 us -> 31.9 us  [swap(): return lax.ppermute(value, everything, swap_pairs(plane, seqs, tps, move))]
    all_to_all x4 -> x3, waiting for transfers between devices: 35.1 us -> 20.4 us  [exchange(): return lax.all_to_all(value, names, split_axis=0, concat_axis=0, tiled=True)]
    pallas_call x6 -> x7, Pallas kernels: 27.4 us -> 15 us  [call(): pl.pallas_call(body, out_shape=outs, in_specs=whole(*arrays), out_specs=j...]
    all_to_all x0 -> x1, blocking collectives: none -> 12.1 us  [exchange(): return lax.all_to_all(value, names, split_axis=0, concat_axis=0, tiled=True)]
    all_to_all x4 -> x3, starting transfers between devices: 19 us -> 13.7 us  [exchange(): return lax.all_to_all(value, names, split_axis=0, concat_axis=0, tiled=True)]
    another operation x3 -> x0, other arithmetic: 1.82 us -> none  [the longest x1 0.66 us: fast_local(): jnp.stack([quarter(1 - x, 1 - s), between[0], between[1], quarter(x, s)])]
    ppermute x11, starting transfers between devices: 7.44 us -> 9.05 us  [swap(): return lax.ppermute(value, everything, swap_pairs(plane, seqs, tps, move))]
    slice x2 -> x0, local copies, waits for them, and re-layouts: 1.58 us -> none  [the longest x1 0.85 us: fast_local(): kept[half:]]
  transfers between devices with their start and end apart: 15 -> 14, of which waited for: 6 -> 7; matrix products, arithmetic and copies ran while one was open for 6% -> 0% of each run, Pallas kernels for 22% -> 15%
where the time goes in v3:
time: 128 us; the launch traced here: 127 us
  waiting for transfers between devices  52.3 us (41%)
  Pallas kernels  31.4 us (25%)
  starting transfers between devices  22.8 us (18%)
  blocking collectives  12.1 us (9%)
  local copies, waits for them, and re-layouts  7.53 us (6%)
    ppermute x11, waiting for transfers between devices, swap(): return lax.ppermute(value, everything, swap_pairs(plane, seqs, tps, move))  31.9 us
    all_to_all x3, waiting for transfers between devices, exchange(): return lax.all_to_all(value, names, split_axis=0, concat_axis=0, tiled=True)  20.4 us
    pallas_call x7, Pallas kernels, call(): pl.pallas_call(body, out_shape=outs, in_specs=whole(*arrays), out_specs=j...  15 us
    all_to_all x3, starting transfers between devices, exchange(): return lax.all_to_all(value, names, split_axis=0, concat_axis=0, tiled=True)  13.7 us
    all_to_all x1, blocking collectives, exchange(): return lax.all_to_all(value, names, split_axis=0, concat_axis=0, tiled=True)  12.1 us
    ppermute x11, starting transfers between devices, swap(): return lax.ppermute(value, everything, swap_pairs(plane, seqs, tps, move))  9.05 us
    unnamed x22, local copies, waits for them, and re-layouts  7.41 us
    pallas_call x1, Pallas kernels, prompt_visual(): pl.pallas_call(body, grid=(tokens // block,), out_shape=jax.ShapeDtypeStr...  6.61 us
  transfers between devices with their start and end apart: 14, of which 7 were waited for; matrix products, arithmetic and copies ran while one was open for 0% of the time, Pallas kernels for 15%

profile of v3, /device:TPU:0, one launch (start us, length us, event | category | flops | bytes accessed | tf_op | source)
XLA Modules:
  0.0 127.0 jit_solution(8178517120047422599)
XLA Ops:
  0.5 1.3 %copy-done.6 = bf16[1,64,3,1280]{3,1,2,0:T(8,128)(2,1)S(1)} copy-done((bf16[1,64,3,1280]{3,1,2,0:T(8,128)(2,1)S(1)}, bf16[1,64,3,1280]{3,1,2,0:T(8,128)(2,1)}, u32[]{:S(2)}) %copy-start.6) | copy-done | bytes 491544
  3.2 6.7 %all-to-all-start = ((bf16[8,64,480]{2,1,0:T(8,128)(2,1)}), bf16[8,64,480]{2,1,0:T(8,128)(2,1)}, u32[]{:S(2)}, u32[]{:S(2)}) async-start(bf16[8,64,480]{2,1,0:T(8,128)(2,1)} %copy-done.2), calls=%async_computation | async-start | bytes 1048576 | tf_op jit(solution)/shard_map/all_to_all | solution.py:570
  9.9 1.5 %collective-permute-start.3 = (bf16[2048,256]{1,0:T(8,128)(2,1)}, bf16[2048,256]{1,0:T(8,128)(2,1)}, u32[]{:S(2)}, u32[]{:S(2)}) collective-permute-start(bf16[2048,256]{1,0:T(8,128)(2,1)} %refs_0_.1), channel_id=1, source_target_pairs={{0,16},{1,17},{2,18},{3,19},{4,20},{5,21},{6,22},{7,23},{8,12},{9,... | collective-permute-start | bytes 3145736 | tf_op jit(solution)/shard_map/ppermute | solution.py:567
  12.2 14.0 %all-to-all-done.spread_ref = bf16[8,64,480]{2,1,0:T(8,128)(2,1)} async-done(((bf16[8,64,480]{2,1,0:T(8,128)(2,1)}), bf16[8,64,480]{2,1,0:T(8,128)(2,1)}, u32[]{:S(2)}, u32[]{:S(2)}) %all-to-all-start) | async-done | bytes 491552 | tf_op jit(solution)/shard_map/all_to_all | solution.py:570
  26.3 4.0 %shard_map.92 = bf16[8,80,128]{2,1,0:T(8,128)(2,1)S(1)} custom-call(s32[26]{0:T(128)S(1)} %stack.97.scalars_ref, bf16[8,64,480]{2,1,0:T(8,128)(2,1)} %all-to-all-done.spread_ref), custom_call_target="tpu_custom_call" | custom-call | tf_op jit(solution)/shard_map/pallas_call | solution.py:192
  30.9 3.4 %all-to-all-start.1 = ((bf16[8,80,128]{2,1,0:T(8,128)(2,1)}), bf16[8,80,128]{2,1,0:T(8,128)(2,1)S(1)}, u32[]{:S(2)}, u32[]{:S(2)}) async-start(bf16[8,80,128]{2,1,0:T(8,128)(2,1)} %copy-done.5), calls=%async_computation.1 | async-start | bytes 327680 | tf_op jit(solution)/shard_map/all_to_all | solution.py:570
  34.3 1.9 %collective-permute-start.4 = (bf16[2048,256]{1,0:T(8,128)(2,1)}, bf16[2048,256]{1,0:T(8,128)(2,1)}, u32[]{:S(2)}, u32[]{:S(2)}) collective-permute-start(bf16[2048,256]{1,0:T(8,128)(2,1)} %refs_0_.1), channel_id=1, source_target_pairs={{0,4},{1,5},{2,6},{3,7},{4,0},{5,1},{6,2},{7,3},{8,24},{9,25},{10,... | collective-permute-start | bytes 3145736 | tf_op jit(solution)/shard_map/ppermute | solution.py:567
  36.4 6.0 %all-to-all-done.1.returned_ref = bf16[8,80,128]{2,1,0:T(8,128)(2,1)S(1)} async-done(((bf16[8,80,128]{2,1,0:T(8,128)(2,1)}), bf16[8,80,128]{2,1,0:T(8,128)(2,1)S(1)}, u32[]{:S(2)}, u32[]{:S(2)}) %all-to-all-start.1) | async-done | bytes 163872 | tf_op jit(solution)/shard_map/all_to_all | solution.py:570
  42.4 1.6 %shard_map.93 = bf16[16,16,1280]{2,1,0:T(8,128)(2,1)S(1)} custom-call(s32[26]{0:T(128)S(1)} %stack.97.scalars_ref, bf16[8,80,128]{2,1,0:T(8,128)(2,1)S(1)} %all-to-all-done.1.returned_ref, bf16[1280,1280]{1,0:T(8,128)(2,1)S(1)} %copy-done, f32[1,1280]{1,0:T(1,128)S(1)} %broadcast_in_dim.9.gain_ref), custom_call_target="tpu_custom_call" | custom-call | tf_op jit(solution)/shard_map/pallas_call | solution.py:192
  44.9 3.6 %all-to-all-start.2 = ((bf16[16,16,1280]{2,1,0:T(8,128)(2,1)}), bf16[16,16,1280]{2,1,0:T(8,128)(2,1)S(1)}, u32[]{:S(2)}, u32[]{:S(2)}) async-start(bf16[16,16,1280]{2,1,0:T(8,128)(2,1)} %copy-done.1), calls=%async_computation.2 | async-start | bytes 1310720 | tf_op jit(solution)/shard_map/all_to_all | solution.py:570
  49.0 2.0 %collective-permute-done.4.refs_2_ = bf16[2048,256]{1,0:T(8,128)(2,1)} collective-permute-done((bf16[2048,256]{1,0:T(8,128)(2,1)}, bf16[2048,256]{1,0:T(8,128)(2,1)}, u32[]{:S(2)}, u32[]{:S(2)}) %collective-permute-start.4) | collective-permute-done | bytes 1048608 | tf_op jit(solution)/shard_map/ppermute | solution.py:567
  51.1 17.4 %collective-permute-done.5.refs_3_ = bf16[2048,256]{1,0:T(8,128)(2,1)} collective-permute-done((bf16[2048,256]{1,0:T(8,128)(2,1)}, bf16[2048,256]{1,0:T(8,128)(2,1)}, u32[]{:S(2)}, u32[]{:S(2)}) %collective-permute-start.5) | collective-permute-done | bytes 1048608 | tf_op jit(solution)/shard_map/ppermute | solution.py:567
  68.8 4.5 %shard_map.94 = (bf16[128,2048]{1,0:T(8,128)(2,1)S(1)}, f32[128,2048]{1,0:T(8,128)S(1)}) custom-call(s32[26]{0:T(128)S(1)} %stack.97.scalars_ref, bf16[4,64,1280]{2,1,0:T(8,128)(2,1)S(1)} %bitcast.36, bf16[640,2048]{1,0:T(8,128)(2,1)} %own_ref.1, bf16[640,2048]{1,0:T(8,128)(2,1)} %collective-permute-done.other_ref), custom_call_target="tpu_custom_call" | custom-call | tf_op jit(solution)/shard_map/pallas_call | solution.py:336
  73.3 1.6 %collective-permute-start.1 = (bf16[128,2048]{1,0:T(8,128)(2,1)S(1)}, bf16[128,2048]{1,0:T(8,128)(2,1)S(1)}, u32[]{:S(2)}, u32[]{:S(2)}) collective-permute-start(bf16[128,2048]{1,0:T(8,128)(2,1)S(1)} %get-tuple-element.14), channel_id=1, source_target_pairs={{0,16},{1,17},{2,18},{3,19},{4,20},{5,21},{6,22},{7,23},{8,12},{9,... | collective-permute-start | bytes 1572872 | tf_op jit(solution)/shard_map/ppermute | solution.py:567
  74.9 7.7 %collective-permute-done.1.received_ref = bf16[128,2048]{1,0:T(8,128)(2,1)S(1)} collective-permute-done((bf16[128,2048]{1,0:T(8,128)(2,1)S(1)}, bf16[128,2048]{1,0:T(8,128)(2,1)S(1)}, u32[]{:S(2)}, u32[]{:S(2)}) %collective-permute-start.1) | collective-permute-done | bytes 524320 | tf_op jit(solution)/shard_map/ppermute | solution.py:567
  82.7 1.6 %collective-permute-start.2 = (bf16[64,2048]{1,0:T(8,128)(2,1)S(1)}, bf16[64,2048]{1,0:T(8,128)(2,1)S(1)}, u32[]{:S(2)}, u32[]{:S(2)}) collective-permute-start(bf16[64,2048]{1,0:T(8,128)(2,1)S(1)} %get-tuple-element.16), channel_id=1, source_target_pairs={{0,4},{1,5},{2,6},{3,7},{4,0},{5,1},{6,2},{7,3},{8,24},{9,25},{10,... | collective-permute-start | bytes 786440 | tf_op jit(solution)/shard_map/ppermute | solution.py:567
  84.3 4.8 %collective-permute-done.2.received_ref = bf16[64,2048]{1,0:T(8,128)(2,1)S(1)} collective-permute-done((bf16[64,2048]{1,0:T(8,128)(2,1)S(1)}, bf16[64,2048]{1,0:T(8,128)(2,1)S(1)}, u32[]{:S(2)}, u32[]{:S(2)}) %collective-permute-start.2) | collective-permute-done | bytes 262176 | tf_op jit(solution)/shard_map/ppermute | solution.py:567
  89.1 5.3 %shard_map.96 = bf16[4,144,256]{2,1,0:T(8,128)(2,1)S(1)} custom-call(s32[26]{0:T(128)S(1)} %stack.97.scalars_ref, f32[64,2048]{1,0:T(8,128)S(1)} %get-tuple-element.15.kept_ref, bf16[64,2048]{1,0:T(8,128)(2,1)S(1)} %collective-permute-done.2.received_ref, f32[1,2048]{1,0:T(1,128)S(1)} %bitcast.38, bf16[2048,256]{1,0:T(8,128)(2,1)} %refs_0_.1, ...), custom_call_target="tpu_custom_call" | custom-call | tf_op jit(solution)/shard_map/pallas_call | solution.py:401
  94.4 12.1 %all_to_all.20.sums_ref = bf16[4,144,256]{2,1,0:T(8,128)(2,1)S(1)} all-to-all(bf16[4,144,256]{2,1,0:T(8,128)(2,1)S(1)} %shard_map.96), channel_id=1, replica_groups=mesh['x'=2,'c'=2,'seq'=2,'tp'=4] {'tp'}, dimensions={0} | all-to-all | bytes 589824 | tf_op jit(solution)/shard_map/all_to_all | solution.py:570
  108.0 4.3 %shard_map.98 = (f32[128,4096]{1,0:T(8,128)S(1)}, f32[2,4096]{1,0:T(2,128)S(1)}) custom-call(bf16[512,16,128]{2,1,0:T(8,128)(2,1)} %bitcast.39, bf16[512,2,2,128]{3,2,1,0:T(2,128)(2,1)} %bitcast.42), custom_call_target="tpu_custom_call" | custom-call | tf_op jit(solution)/shard_map/pallas_call | solution.py:192
  112.2 1.3 %copy-done.3 = f32[128,4096]{1,0:T(8,128)} copy-done((f32[128,4096]{1,0:T(8,128)}, f32[128,4096]{1,0:T(8,128)S(1)}, u32[]{:S(2)}) %copy-start.3) | copy-done | bytes 2097176
  114.2 4.3 %shard_map.99 = (f32[128,4096]{1,0:T(8,128)S(1)}, f32[2,4096]{1,0:T(2,128)S(1)}) custom-call(bf16[512,16,128]{2,1,0:T(8,128)(2,1)} %bitcast.40, bf16[512,2,2,128]{3,2,1,0:T(2,128)(2,1)} %bitcast.43), custom_call_target="tpu_custom_call" | custom-call | tf_op jit(solution)/shard_map/pallas_call | solution.py:192
  118.5 1.3 %copy-done.4 = f32[128,4096]{1,0:T(8,128)} copy-done((f32[128,4096]{1,0:T(8,128)}, f32[128,4096]{1,0:T(8,128)S(1)}, u32[]{:S(2)}) %copy-start.4) | copy-done | bytes 2097176
  120.4 6.6 %shard_map.100 = bf16[512,16,128]{2,1,0:T(8,128)(2,1)} custom-call(s32[26]{0:T(128)S(1)} %stack.97.scalars_ref, bf16[512,16,128]{2,1,0:T(8,128)(2,1)} %bitcast.41, bf16[128,256]{1,0:T(8,128)(2,1)S(1)} %shard_map.97.own_ref, bf16[128,256]{1,0:T(8,128)(2,1)S(1)} %collective-permute-done.10.twin_ref, f32[128,4096]{1,0:T(8,128)} %copy-done.3, ...), custom_call_target="tpu_custom_call" | custom-call | tf_op jit(solution)/shard_map/pallas_call | solution.py:522
  (39 shorter events, 7.3 us)
Async XLA Ops:
  0.0 42.4 %copy-start = (bf16[1280,1280]{1,0:T(8,128)(2,1)S(1)}, bf16[1280,1280]{1,0:T(8,128)(2,1)}, u32[]{:S(2)}) copy-start(bf16[1280,1280]{1,0:T(8,128)(2,1)} %weight_ref.1) | copy-start | bytes 9830404
  0.0 68.8 %collective-permute-start = (bf16[640,2048]{1,0:T(8,128)(2,1)}, bf16[640,2048]{1,0:T(8,128)(2,1)}, u32[]{:S(2)}, u32[]{:S(2)}) collective-permute-start(bf16[640,2048]{1,0:T(8,128)(2,1)} %own_ref.1), channel_id=1, source_target_pairs={{0,8},{1,9},{2,10},{3,11},{4,12},{5,13},{6,14},{7,15},{8,0},{9,1},... | collective-permute-start | bytes 7864328 | tf_op jit(solution)/shard_map/ppermute | solution.py:567
  0.5 1.3 %copy-start.6 = (bf16[1,64,3,1280]{3,1,2,0:T(8,128)(2,1)S(1)}, bf16[1,64,3,1280]{3,1,2,0:T(8,128)(2,1)}, u32[]{:S(2)}) copy-start(bf16[1,64,3,1280]{3,1,2,0:T(8,128)(2,1)} %param.9) | copy-start | bytes 1474564
  1.8 34.6 %copy-start.10 = (f32[1280]{0:T(1024)S(1)}, f32[1280]{0:T(1024)}, u32[]{:S(2)}) copy-start(f32[1280]{0:T(1024)} %param.12) | copy-start | bytes 15364
  2.4 0.8 copy-start.2
  3.2 23.1 %all-to-all-start = ((bf16[8,64,480]{2,1,0:T(8,128)(2,1)}), bf16[8,64,480]{2,1,0:T(8,128)(2,1)}, u32[]{:S(2)}, u32[]{:S(2)}) async-start(bf16[8,64,480]{2,1,0:T(8,128)(2,1)} %copy-done.2), calls=%async_computation | async-start | bytes 1048576 | tf_op jit(solution)/shard_map/all_to_all | solution.py:570
  9.9 26.3 %collective-permute-start.3 = (bf16[2048,256]{1,0:T(8,128)(2,1)}, bf16[2048,256]{1,0:T(8,128)(2,1)}, u32[]{:S(2)}, u32[]{:S(2)}) collective-permute-start(bf16[2048,256]{1,0:T(8,128)(2,1)} %refs_0_.1), channel_id=1, source_target_pairs={{0,16},{1,17},{2,18},{3,19},{4,20},{5,21},{6,22},{7,23},{8,12},{9,... | collective-permute-start | bytes 3145736 | tf_op jit(solution)/shard_map/ppermute | solution.py:567
  30.2 0.7 copy-start.5
  30.9 11.5 %all-to-all-start.1 = ((bf16[8,80,128]{2,1,0:T(8,128)(2,1)}), bf16[8,80,128]{2,1,0:T(8,128)(2,1)S(1)}, u32[]{:S(2)}, u32[]{:S(2)}) async-start(bf16[8,80,128]{2,1,0:T(8,128)(2,1)} %copy-done.5), calls=%async_computation.1 | async-start | bytes 327680 | tf_op jit(solution)/shard_map/all_to_all | solution.py:570
  34.3 16.8 %collective-permute-start.4 = (bf16[2048,256]{1,0:T(8,128)(2,1)}, bf16[2048,256]{1,0:T(8,128)(2,1)}, u32[]{:S(2)}, u32[]{:S(2)}) collective-permute-start(bf16[2048,256]{1,0:T(8,128)(2,1)} %refs_0_.1), channel_id=1, source_target_pairs={{0,4},{1,5},{2,6},{3,7},{4,0},{5,1},{6,2},{7,3},{8,24},{9,25},{10,... | collective-permute-start | bytes 3145736 | tf_op jit(solution)/shard_map/ppermute | solution.py:567
  36.2 32.2 %collective-permute-start.5 = (bf16[2048,256]{1,0:T(8,128)(2,1)}, bf16[2048,256]{1,0:T(8,128)(2,1)}, u32[]{:S(2)}, u32[]{:S(2)}) collective-permute-start(bf16[2048,256]{1,0:T(8,128)(2,1)} %collective-permute-done.3.refs_1_), channel_id=1, source_target_pairs={{0,4},{1,5},{2,6},{3,7},{4,0},{5,1},{6,2},{7,3},{8,24},{9,25},{10,... | collective-permute-start | bytes 3145736 | tf_op jit(solution)/shard_map/ppermute | solution.py:567
  44.0 0.8 copy-start.1
  44.9 23.9 %all-to-all-start.2 = ((bf16[16,16,1280]{2,1,0:T(8,128)(2,1)}), bf16[16,16,1280]{2,1,0:T(8,128)(2,1)S(1)}, u32[]{:S(2)}, u32[]{:S(2)}) async-start(bf16[16,16,1280]{2,1,0:T(8,128)(2,1)} %copy-done.1), calls=%async_computation.2 | async-start | bytes 1310720 | tf_op jit(solution)/shard_map/all_to_all | solution.py:570
  48.5 35.8 %collective-permute-start.6 = (bf16[2048,256]{1,0:T(8,128)(2,1)}, bf16[2048,256]{1,0:T(8,128)(2,1)}, u32[]{:S(2)}, u32[]{:S(2)}) collective-permute-start(bf16[2048,256]{1,0:T(8,128)(2,1)} %refs_0_.1), channel_id=1, source_target_pairs={{0,8},{1,9},{2,10},{3,11},{4,12},{5,13},{6,14},{7,15},{8,0},{9,1},... | collective-permute-start | bytes 3145736 | tf_op jit(solution)/shard_map/ppermute | solution.py:567
  48.5 35.7 %collective-permute-start.7 = (bf16[2048,256]{1,0:T(8,128)(2,1)}, bf16[2048,256]{1,0:T(8,128)(2,1)}, u32[]{:S(2)}, u32[]{:S(2)}) collective-permute-start(bf16[2048,256]{1,0:T(8,128)(2,1)} %collective-permute-done.3.refs_1_), channel_id=1, source_target_pairs={{0,8},{1,9},{2,10},{3,11},{4,12},{5,13},{6,14},{7,15},{8,0},{9,1},... | collective-permute-start | bytes 3145736 | tf_op jit(solution)/shard_map/ppermute | solution.py:567
  51.1 33.2 %collective-permute-start.8 = (bf16[2048,256]{1,0:T(8,128)(2,1)}, bf16[2048,256]{1,0:T(8,128)(2,1)}, u32[]{:S(2)}, u32[]{:S(2)}) collective-permute-start(bf16[2048,256]{1,0:T(8,128)(2,1)} %collective-permute-done.4.refs_2_), channel_id=1, source_target_pairs={{0,8},{1,9},{2,10},{3,11},{4,12},{5,13},{6,14},{7,15},{8,0},{9,1},... | collective-permute-start | bytes 3145736 | tf_op jit(solution)/shard_map/ppermute | solution.py:567
  68.5 15.9 %collective-permute-start.9 = (bf16[2048,256]{1,0:T(8,128)(2,1)}, bf16[2048,256]{1,0:T(8,128)(2,1)}, u32[]{:S(2)}, u32[]{:S(2)}) collective-permute-start(bf16[2048,256]{1,0:T(8,128)(2,1)} %collective-permute-done.5.refs_3_), channel_id=1, source_target_pairs={{0,8},{1,9},{2,10},{3,11},{4,12},{5,13},{6,14},{7,15},{8,0},{9,1},... | collective-permute-start | bytes 3145736 | tf_op jit(solution)/shard_map/ppermute | solution.py:567
  68.8 20.3 %copy-start.9 = (f32[2048]{0:T(1024)S(1)}, f32[2048]{0:T(1024)}, u32[]{:S(2)}) copy-start(f32[2048]{0:T(1024)} %param.14) | copy-start | bytes 24580
  73.3 9.2 %collective-permute-start.1 = (bf16[128,2048]{1,0:T(8,128)(2,1)S(1)}, bf16[128,2048]{1,0:T(8,128)(2,1)S(1)}, u32[]{:S(2)}, u32[]{:S(2)}) collective-permute-start(bf16[128,2048]{1,0:T(8,128)(2,1)S(1)} %get-tuple-element.14), channel_id=1, source_target_pairs={{0,16},{1,17},{2,18},{3,19},{4,20},{5,21},{6,22},{7,23},{8,12},{9,... | collective-permute-start | bytes 1572872 | tf_op jit(solution)/shard_map/ppermute | solution.py:567
  82.7 6.4 %collective-permute-start.2 = (bf16[64,2048]{1,0:T(8,128)(2,1)S(1)}, bf16[64,2048]{1,0:T(8,128)(2,1)S(1)}, u32[]{:S(2)}, u32[]{:S(2)}) collective-permute-start(bf16[64,2048]{1,0:T(8,128)(2,1)S(1)} %get-tuple-element.16), channel_id=1, source_target_pairs={{0,4},{1,5},{2,6},{3,7},{4,0},{5,1},{6,2},{7,3},{8,24},{9,25},{10,... | collective-permute-start | bytes 786440 | tf_op jit(solution)/shard_map/ppermute | solution.py:567
  106.7 13.6 %collective-permute-start.10 = (bf16[128,256]{1,0:T(8,128)(2,1)S(1)}, bf16[128,256]{1,0:T(8,128)(2,1)S(1)}, u32[]{:S(2)}, u32[]{:S(2)}) collective-permute-start(bf16[128,256]{1,0:T(8,128)(2,1)S(1)} %shard_map.97.own_ref), channel_id=1, source_target_pairs={{0,4},{1,5},{2,6},{3,7},{4,0},{5,1},{6,2},{7,3},{8,12},{9,13},{10,... | collective-permute-start | bytes 196616 | tf_op jit(solution)/shard_map/ppermute | solution.py:567
  112.2 1.3 %copy-start.3 = (f32[128,4096]{1,0:T(8,128)}, f32[128,4096]{1,0:T(8,128)S(1)}, u32[]{:S(2)}) copy-start(f32[128,4096]{1,0:T(8,128)S(1)} %get-tuple-element.17.refs_0_) | copy-start | bytes 6291460
  118.4 1.3 %copy-start.4 = (f32[128,4096]{1,0:T(8,128)}, f32[128,4096]{1,0:T(8,128)S(1)}, u32[]{:S(2)}) copy-start(f32[128,4096]{1,0:T(8,128)S(1)} %get-tuple-element.19.refs_2_) | copy-start | bytes 6291460
  119.8 0.6 copy-start.8
  (1 other events, 0.6 us)

commit v4 on v3

--- a/solution.py
+++ b/solution.py
@@ -211,7 +211,7 @@
                     :, owner * share : (owner + 1) * share
                 ]
 
-    return call(body, jax.ShapeDtypeStruct((owners, patches, kinds * share), rows.dtype), rows)
+    return call(body, pltpu.HBM((owners, patches, kinds * share), rows.dtype), rows)
 
 
 def vision_attention(spread, scalars):
@@ -257,7 +257,7 @@
                     [piece[k * tail_rows : (k + 1) * tail_rows, lanes:] for k in range(folds)], axis=1
                 ).astype(jnp.bfloat16)
 
-    out = jax.ShapeDtypeStruct((owners, patches + tail_rows, lanes), jnp.bfloat16)
+    out = pltpu.HBM((owners, patches + tail_rows, lanes), jnp.bfloat16)
     return call(body, out, scalars, spread, stay=(1,))
 
 
@@ -309,7 +309,7 @@
                     out_ref[place, :, :rows_local] = first[:, cut]
                     out_ref[place, :, rows_local:] = second[:, cut]
 
-    out = jax.ShapeDtypeStruct((plane * seqs * tps, token_rows, 2 * rows_local), jnp.bfloat16)
+    out = pltpu.HBM((plane * seqs * tps, token_rows, 2 * rows_local), jnp.bfloat16)
     return call(
         body, out, scalars, returned, out_weight, gain[None],
         scratch=[pltpu.VMEM((tiles, patches, lanes), jnp.float32)],
@@ -470,8 +470,8 @@
             )
 
     outs = (
-        jax.ShapeDtypeStruct((width, tokens * groups), jnp.float32),
-        jax.ShapeDtypeStruct((2, tokens * groups), jnp.float32),
+        pltpu.HBM((width, tokens * groups), jnp.float32),
+        pltpu.HBM((2, tokens * groups), jnp.float32),
     )
     return call(body, outs, offchip(queries), offchip(span_kv), mib=24)
 

time: 128 us -> 126 us (0.984)
  local copies, waits for them, and re-layouts: 7.53 us -> 1.4 us
  Pallas kernels: 31.4 us -> 36.3 us
    unnamed x22 -> x8, local copies, waits for them, and re-layouts: 7.41 us -> 1.28 us
    pallas_call x7, Pallas kernels: 15 us -> 19.9 us  [call(): pl.pallas_call(body, out_shape=outs, in_specs=whole(*arrays), out_specs=j...]
  transfers between devices with their start and end apart: 14 -> 14, of which waited for: 7 -> 7; matrix products, arithmetic and copies ran while one was open for 0% -> 0% of each run, Pallas kernels for 15% -> 19%
where the time goes in v4:
time: 126 us
  waiting for transfers between devices  52.3 us (42%)
  Pallas kernels  36.3 us (29%)
  starting transfers between devices  22.8 us (18%)
  blocking collectives  12.1 us (10%)
  local copies, waits for them, and re-layouts  1.4 us (1%)
    ppermute x11, waiting for transfers between devices, swap(): return lax.ppermute(value, everything, swap_pairs(plane, seqs, tps, move))  31.9 us
    all_to_all x3, waiting for transfers between devices, exchange(): return lax.all_to_all(value, names, split_axis=0, concat_axis=0, tiled=True)  20.4 us
    pallas_call x7, Pallas kernels, call(): pl.pallas_call(body, out_shape=outs, in_specs=whole(*arrays), out_specs=j...  19.9 us
    all_to_all x3, starting transfers between devices, exchange(): return lax.all_to_all(value, names, split_axis=0, concat_axis=0, tiled=True)  13.7 us
    all_to_all x1, blocking collectives, exchange(): return lax.all_to_all(value, names, split_axis=0, concat_axis=0, tiled=True)  12.1 us
    ppermute x11, starting transfers between devices, swap(): return lax.ppermute(value, everything, swap_pairs(plane, seqs, tps, move))  9.07 us
    pallas_call x1, Pallas kernels, prompt_visual(): pl.pallas_call(body, grid=(tokens // block,), out_shape=jax.ShapeDtypeStr...  6.61 us
    pallas_call x1, Pallas kernels, project_visual(): pl.pallas_call(body, out_shape=out, in_specs=[pl.BlockSpec(memory_space=p...  5.32 us
  transfers between devices with their start and end apart: 14, of which 7 were waited for; matrix products, arithmetic and copies ran while one was open for 0% of the time, Pallas kernels for 19%

profile of v4, /device:TPU:0, one launch (start us, length us, event | category | flops | bytes accessed | tf_op | source)
XLA Modules:
  0.0 125.7 jit_solution(14269670073757072160)
XLA Ops:
  0.5 1.3 %copy-done.1 = bf16[1,64,3,1280]{3,1,2,0:T(8,128)(2,1)S(1)} copy-done((bf16[1,64,3,1280]{3,1,2,0:T(8,128)(2,1)S(1)}, bf16[1,64,3,1280]{3,1,2,0:T(8,128)(2,1)}, u32[]{:S(2)}) %copy-start.1) | copy-done | bytes 491544
  1.8 1.4 %shard_map.91 = bf16[8,64,480]{2,1,0:T(8,128)(2,1)} custom-call(bf16[3,64,1280]{2,1,0:T(8,128)(2,1)S(1)} %bitcast.37), custom_call_target="tpu_custom_call" | custom-call | tf_op jit(solution)/shard_map/pallas_call | solution.py:192
  3.2 6.7 %all-to-all-start = ((bf16[8,64,480]{2,1,0:T(8,128)(2,1)}), bf16[8,64,480]{2,1,0:T(8,128)(2,1)}, u32[]{:S(2)}, u32[]{:S(2)}) async-start(bf16[8,64,480]{2,1,0:T(8,128)(2,1)} %shard_map.91), calls=%async_computation | async-start | bytes 1048576 | tf_op jit(solution)/shard_map/all_to_all | solution.py:570
  9.9 1.5 %collective-permute-start.3 = (bf16[2048,256]{1,0:T(8,128)(2,1)}, bf16[2048,256]{1,0:T(8,128)(2,1)}, u32[]{:S(2)}, u32[]{:S(2)}) collective-permute-start(bf16[2048,256]{1,0:T(8,128)(2,1)} %refs_0_.1), channel_id=1, source_target_pairs={{0,16},{1,17},{2,18},{3,19},{4,20},{5,21},{6,22},{7,23},{8,12},{9,... | collective-permute-start | bytes 3145736 | tf_op jit(solution)/shard_map/ppermute | solution.py:567
  12.2 14.0 %all-to-all-done.spread_ref = bf16[8,64,480]{2,1,0:T(8,128)(2,1)} async-done(((bf16[8,64,480]{2,1,0:T(8,128)(2,1)}), bf16[8,64,480]{2,1,0:T(8,128)(2,1)}, u32[]{:S(2)}, u32[]{:S(2)}) %all-to-all-start) | async-done | bytes 491552 | tf_op jit(solution)/shard_map/all_to_all | solution.py:570
  26.3 4.6 %shard_map.92 = bf16[8,80,128]{2,1,0:T(8,128)(2,1)} custom-call(s32[26]{0:T(128)S(1)} %stack.97.scalars_ref, bf16[8,64,480]{2,1,0:T(8,128)(2,1)} %all-to-all-done.spread_ref), custom_call_target="tpu_custom_call" | custom-call | tf_op jit(solution)/shard_map/pallas_call | solution.py:192
  30.9 3.4 %all-to-all-start.1 = ((bf16[8,80,128]{2,1,0:T(8,128)(2,1)}), bf16[8,80,128]{2,1,0:T(8,128)(2,1)S(1)}, u32[]{:S(2)}, u32[]{:S(2)}) async-start(bf16[8,80,128]{2,1,0:T(8,128)(2,1)} %shard_map.92), calls=%async_computation.1 | async-start | bytes 327680 | tf_op jit(solution)/shard_map/all_to_all | solution.py:570
  34.3 1.9 %collective-permute-start.4 = (bf16[2048,256]{1,0:T(8,128)(2,1)}, bf16[2048,256]{1,0:T(8,128)(2,1)}, u32[]{:S(2)}, u32[]{:S(2)}) collective-permute-start(bf16[2048,256]{1,0:T(8,128)(2,1)} %refs_0_.1), channel_id=1, source_target_pairs={{0,4},{1,5},{2,6},{3,7},{4,0},{5,1},{6,2},{7,3},{8,24},{9,25},{10,... | collective-permute-start | bytes 3145736 | tf_op jit(solution)/shard_map/ppermute | solution.py:567
  36.4 6.0 %all-to-all-done.1.returned_ref = bf16[8,80,128]{2,1,0:T(8,128)(2,1)S(1)} async-done(((bf16[8,80,128]{2,1,0:T(8,128)(2,1)}), bf16[8,80,128]{2,1,0:T(8,128)(2,1)S(1)}, u32[]{:S(2)}, u32[]{:S(2)}) %all-to-all-start.1) | async-done | bytes 163872 | tf_op jit(solution)/shard_map/all_to_all | solution.py:570
  42.4 2.4 %shard_map.93 = bf16[16,16,1280]{2,1,0:T(8,128)(2,1)} custom-call(s32[26]{0:T(128)S(1)} %stack.97.scalars_ref, bf16[8,80,128]{2,1,0:T(8,128)(2,1)S(1)} %all-to-all-done.1.returned_ref, bf16[1280,1280]{1,0:T(8,128)(2,1)S(1)} %copy-done, f32[1,1280]{1,0:T(1,128)S(1)} %broadcast_in_dim.9.gain_ref), custom_call_target="tpu_custom_call" | custom-call | tf_op jit(solution)/shard_map/pallas_call | solution.py:192
  44.8 3.6 %all-to-all-start.2 = ((bf16[16,16,1280]{2,1,0:T(8,128)(2,1)}), bf16[16,16,1280]{2,1,0:T(8,128)(2,1)S(1)}, u32[]{:S(2)}, u32[]{:S(2)}) async-start(bf16[16,16,1280]{2,1,0:T(8,128)(2,1)} %shard_map.93), calls=%async_computation.2 | async-start | bytes 1310720 | tf_op jit(solution)/shard_map/all_to_all | solution.py:570
  49.0 2.0 %collective-permute-done.4.refs_2_ = bf16[2048,256]{1,0:T(8,128)(2,1)} collective-permute-done((bf16[2048,256]{1,0:T(8,128)(2,1)}, bf16[2048,256]{1,0:T(8,128)(2,1)}, u32[]{:S(2)}, u32[]{:S(2)}) %collective-permute-start.4) | collective-permute-done | bytes 1048608 | tf_op jit(solution)/shard_map/ppermute | solution.py:567
  51.1 17.4 %collective-permute-done.5.refs_3_ = bf16[2048,256]{1,0:T(8,128)(2,1)} collective-permute-done((bf16[2048,256]{1,0:T(8,128)(2,1)}, bf16[2048,256]{1,0:T(8,128)(2,1)}, u32[]{:S(2)}, u32[]{:S(2)}) %collective-permute-start.5) | collective-permute-done | bytes 1048608 | tf_op jit(solution)/shard_map/ppermute | solution.py:567
  68.8 4.5 %shard_map.94 = (bf16[128,2048]{1,0:T(8,128)(2,1)S(1)}, f32[128,2048]{1,0:T(8,128)S(1)}) custom-call(s32[26]{0:T(128)S(1)} %stack.97.scalars_ref, bf16[4,64,1280]{2,1,0:T(8,128)(2,1)S(1)} %bitcast.36, bf16[640,2048]{1,0:T(8,128)(2,1)} %own_ref.1, bf16[640,2048]{1,0:T(8,128)(2,1)} %collective-permute-done.other_ref), custom_call_target="tpu_custom_call" | custom-call | tf_op jit(solution)/shard_map/pallas_call | solution.py:336
  73.3 1.6 %collective-permute-start.1 = (bf16[128,2048]{1,0:T(8,128)(2,1)S(1)}, bf16[128,2048]{1,0:T(8,128)(2,1)S(1)}, u32[]{:S(2)}, u32[]{:S(2)}) collective-permute-start(bf16[128,2048]{1,0:T(8,128)(2,1)S(1)} %get-tuple-element.14), channel_id=1, source_target_pairs={{0,16},{1,17},{2,18},{3,19},{4,20},{5,21},{6,22},{7,23},{8,12},{9,... | collective-permute-start | bytes 1572872 | tf_op jit(solution)/shard_map/ppermute | solution.py:567
  74.9 7.7 %collective-permute-done.1.received_ref = bf16[128,2048]{1,0:T(8,128)(2,1)S(1)} collective-permute-done((bf16[128,2048]{1,0:T(8,128)(2,1)S(1)}, bf16[128,2048]{1,0:T(8,128)(2,1)S(1)}, u32[]{:S(2)}, u32[]{:S(2)}) %collective-permute-start.1) | collective-permute-done | bytes 524320 | tf_op jit(solution)/shard_map/ppermute | solution.py:567
  82.7 1.6 %collective-permute-start.2 = (bf16[64,2048]{1,0:T(8,128)(2,1)S(1)}, bf16[64,2048]{1,0:T(8,128)(2,1)S(1)}, u32[]{:S(2)}, u32[]{:S(2)}) collective-permute-start(bf16[64,2048]{1,0:T(8,128)(2,1)S(1)} %get-tuple-element.16), channel_id=1, source_target_pairs={{0,4},{1,5},{2,6},{3,7},{4,0},{5,1},{6,2},{7,3},{8,24},{9,25},{10,... | collective-permute-start | bytes 786440 | tf_op jit(solution)/shard_map/ppermute | solution.py:567
  84.3 4.8 %collective-permute-done.2.received_ref = bf16[64,2048]{1,0:T(8,128)(2,1)S(1)} collective-permute-done((bf16[64,2048]{1,0:T(8,128)(2,1)S(1)}, bf16[64,2048]{1,0:T(8,128)(2,1)S(1)}, u32[]{:S(2)}, u32[]{:S(2)}) %collective-permute-start.2) | collective-permute-done | bytes 262176 | tf_op jit(solution)/shard_map/ppermute | solution.py:567
  89.1 5.3 %shard_map.96 = bf16[4,144,256]{2,1,0:T(8,128)(2,1)S(1)} custom-call(s32[26]{0:T(128)S(1)} %stack.97.scalars_ref, f32[64,2048]{1,0:T(8,128)S(1)} %get-tuple-element.15.kept_ref, bf16[64,2048]{1,0:T(8,128)(2,1)S(1)} %collective-permute-done.2.received_ref, f32[1,2048]{1,0:T(1,128)S(1)} %bitcast.38, bf16[2048,256]{1,0:T(8,128)(2,1)} %refs_0_.1, ...), custom_call_target="tpu_custom_call" | custom-call | tf_op jit(solution)/shard_map/pallas_call | solution.py:401
  94.4 12.1 %all_to_all.20.sums_ref = bf16[4,144,256]{2,1,0:T(8,128)(2,1)S(1)} all-to-all(bf16[4,144,256]{2,1,0:T(8,128)(2,1)S(1)} %shard_map.96), channel_id=1, replica_groups=mesh['x'=2,'c'=2,'seq'=2,'tp'=4] {'tp'}, dimensions={0} | all-to-all | bytes 589824 | tf_op jit(solution)/shard_map/all_to_all | solution.py:570
  106.7 1.2 collective-permute-start.10
  108.0 5.6 %shard_map.98 = (f32[128,4096]{1,0:T(8,128)}, f32[2,4096]{1,0:T(2,128)}) custom-call(bf16[512,16,128]{2,1,0:T(8,128)(2,1)} %bitcast.39, bf16[512,2,2,128]{3,2,1,0:T(2,128)(2,1)} %bitcast.42), custom_call_target="tpu_custom_call" | custom-call | tf_op jit(solution)/shard_map/pallas_call | solution.py:192
  113.5 5.5 %shard_map.99 = (f32[128,4096]{1,0:T(8,128)}, f32[2,4096]{1,0:T(2,128)}) custom-call(bf16[512,16,128]{2,1,0:T(8,128)(2,1)} %bitcast.40, bf16[512,2,2,128]{3,2,1,0:T(2,128)(2,1)} %bitcast.43), custom_call_target="tpu_custom_call" | custom-call | tf_op jit(solution)/shard_map/pallas_call | solution.py:192
  119.1 6.6 %shard_map.100 = bf16[512,16,128]{2,1,0:T(8,128)(2,1)} custom-call(s32[26]{0:T(128)S(1)} %stack.97.scalars_ref, bf16[512,16,128]{2,1,0:T(8,128)(2,1)} %bitcast.41, bf16[128,256]{1,0:T(8,128)(2,1)S(1)} %shard_map.97.own_ref, bf16[128,256]{1,0:T(8,128)(2,1)S(1)} %collective-permute-done.10.twin_ref, f32[128,4096]{1,0:T(8,128)} %get-tuple-element.17.refs_0_, ...), custom_call_target="tpu_custom_call" | custom-call | tf_op jit(solution)/shard_map/pallas_call | solution.py:522
  (25 shorter events, 1.9 us)
Async XLA Ops:
  0.0 42.4 %copy-start = (bf16[1280,1280]{1,0:T(8,128)(2,1)S(1)}, bf16[1280,1280]{1,0:T(8,128)(2,1)}, u32[]{:S(2)}) copy-start(bf16[1280,1280]{1,0:T(8,128)(2,1)} %weight_ref.1) | copy-start | bytes 9830404
  0.0 68.8 %collective-permute-start = (bf16[640,2048]{1,0:T(8,128)(2,1)}, bf16[640,2048]{1,0:T(8,128)(2,1)}, u32[]{:S(2)}, u32[]{:S(2)}) collective-permute-start(bf16[640,2048]{1,0:T(8,128)(2,1)} %own_ref.1), channel_id=1, source_target_pairs={{0,8},{1,9},{2,10},{3,11},{4,12},{5,13},{6,14},{7,15},{8,0},{9,1},... | collective-permute-start | bytes 7864328 | tf_op jit(solution)/shard_map/ppermute | solution.py:567
  0.5 1.3 %copy-start.1 = (bf16[1,64,3,1280]{3,1,2,0:T(8,128)(2,1)S(1)}, bf16[1,64,3,1280]{3,1,2,0:T(8,128)(2,1)}, u32[]{:S(2)}) copy-start(bf16[1,64,3,1280]{3,1,2,0:T(8,128)(2,1)} %param.9) | copy-start | bytes 1474564
  1.8 34.6 %copy-start.3 = (f32[1280]{0:T(1024)S(1)}, f32[1280]{0:T(1024)}, u32[]{:S(2)}) copy-start(f32[1280]{0:T(1024)} %param.12) | copy-start | bytes 15364
  3.2 23.1 %all-to-all-start = ((bf16[8,64,480]{2,1,0:T(8,128)(2,1)}), bf16[8,64,480]{2,1,0:T(8,128)(2,1)}, u32[]{:S(2)}, u32[]{:S(2)}) async-start(bf16[8,64,480]{2,1,0:T(8,128)(2,1)} %shard_map.91), calls=%async_computation | async-start | bytes 1048576 | tf_op jit(solution)/shard_map/all_to_all | solution.py:570
  9.9 26.3 %collective-permute-start.3 = (bf16[2048,256]{1,0:T(8,128)(2,1)}, bf16[2048,256]{1,0:T(8,128)(2,1)}, u32[]{:S(2)}, u32[]{:S(2)}) collective-permute-start(bf16[2048,256]{1,0:T(8,128)(2,1)} %refs_0_.1), channel_id=1, source_target_pairs={{0,16},{1,17},{2,18},{3,19},{4,20},{5,21},{6,22},{7,23},{8,12},{9,... | collective-permute-start | bytes 3145736 | tf_op jit(solution)/shard_map/ppermute | solution.py:567
  30.9 11.5 %all-to-all-start.1 = ((bf16[8,80,128]{2,1,0:T(8,128)(2,1)}), bf16[8,80,128]{2,1,0:T(8,128)(2,1)S(1)}, u32[]{:S(2)}, u32[]{:S(2)}) async-start(bf16[8,80,128]{2,1,0:T(8,128)(2,1)} %shard_map.92), calls=%async_computation.1 | async-start | bytes 327680 | tf_op jit(solution)/shard_map/all_to_all | solution.py:570
  34.3 16.8 %collective-permute-start.4 = (bf16[2048,256]{1,0:T(8,128)(2,1)}, bf16[2048,256]{1,0:T(8,128)(2,1)}, u32[]{:S(2)}, u32[]{:S(2)}) collective-permute-start(bf16[2048,256]{1,0:T(8,128)(2,1)} %refs_0_.1), channel_id=1, source_target_pairs={{0,4},{1,5},{2,6},{3,7},{4,0},{5,1},{6,2},{7,3},{8,24},{9,25},{10,... | collective-permute-start | bytes 3145736 | tf_op jit(solution)/shard_map/ppermute | solution.py:567
  36.2 32.2 %collective-permute-start.5 = (bf16[2048,256]{1,0:T(8,128)(2,1)}, bf16[2048,256]{1,0:T(8,128)(2,1)}, u32[]{:S(2)}, u32[]{:S(2)}) collective-permute-start(bf16[2048,256]{1,0:T(8,128)(2,1)} %collective-permute-done.3.refs_1_), channel_id=1, source_target_pairs={{0,4},{1,5},{2,6},{3,7},{4,0},{5,1},{6,2},{7,3},{8,24},{9,25},{10,... | collective-permute-start | bytes 3145736 | tf_op jit(solution)/shard_map/ppermute | solution.py:567
  44.8 23.9 %all-to-all-start.2 = ((bf16[16,16,1280]{2,1,0:T(8,128)(2,1)}), bf16[16,16,1280]{2,1,0:T(8,128)(2,1)S(1)}, u32[]{:S(2)}, u32[]{:S(2)}) async-start(bf16[16,16,1280]{2,1,0:T(8,128)(2,1)} %shard_map.93), calls=%async_computation.2 | async-start | bytes 1310720 | tf_op jit(solution)/shard_map/all_to_all | solution.py:570
  48.4 35.8 %collective-permute-start.6 = (bf16[2048,256]{1,0:T(8,128)(2,1)}, bf16[2048,256]{1,0:T(8,128)(2,1)}, u32[]{:S(2)}, u32[]{:S(2)}) collective-permute-start(bf16[2048,256]{1,0:T(8,128)(2,1)} %refs_0_.1), channel_id=1, source_target_pairs={{0,8},{1,9},{2,10},{3,11},{4,12},{5,13},{6,14},{7,15},{8,0},{9,1},... | collective-permute-start | bytes 3145736 | tf_op jit(solution)/shard_map/ppermute | solution.py:567
  48.5 35.8 %collective-permute-start.7 = (bf16[2048,256]{1,0:T(8,128)(2,1)}, bf16[2048,256]{1,0:T(8,128)(2,1)}, u32[]{:S(2)}, u32[]{:S(2)}) collective-permute-start(bf16[2048,256]{1,0:T(8,128)(2,1)} %collective-permute-done.3.refs_1_), channel_id=1, source_target_pairs={{0,8},{1,9},{2,10},{3,11},{4,12},{5,13},{6,14},{7,15},{8,0},{9,1},... | collective-permute-start | bytes 3145736 | tf_op jit(solution)/shard_map/ppermute | solution.py:567
  51.1 33.2 %collective-permute-start.8 = (bf16[2048,256]{1,0:T(8,128)(2,1)}, bf16[2048,256]{1,0:T(8,128)(2,1)}, u32[]{:S(2)}, u32[]{:S(2)}) collective-permute-start(bf16[2048,256]{1,0:T(8,128)(2,1)} %collective-permute-done.4.refs_2_), channel_id=1, source_target_pairs={{0,8},{1,9},{2,10},{3,11},{4,12},{5,13},{6,14},{7,15},{8,0},{9,1},... | collective-permute-start | bytes 3145736 | tf_op jit(solution)/shard_map/ppermute | solution.py:567
  68.4 15.9 %collective-permute-start.9 = (bf16[2048,256]{1,0:T(8,128)(2,1)}, bf16[2048,256]{1,0:T(8,128)(2,1)}, u32[]{:S(2)}, u32[]{:S(2)}) collective-permute-start(bf16[2048,256]{1,0:T(8,128)(2,1)} %collective-permute-done.5.refs_3_), channel_id=1, source_target_pairs={{0,8},{1,9},{2,10},{3,11},{4,12},{5,13},{6,14},{7,15},{8,0},{9,1},... | collective-permute-start | bytes 3145736 | tf_op jit(solution)/shard_map/ppermute | solution.py:567
  68.8 20.3 %copy-start.2 = (f32[2048]{0:T(1024)S(1)}, f32[2048]{0:T(1024)}, u32[]{:S(2)}) copy-start(f32[2048]{0:T(1024)} %param.14) | copy-start | bytes 24580
  73.3 9.2 %collective-permute-start.1 = (bf16[128,2048]{1,0:T(8,128)(2,1)S(1)}, bf16[128,2048]{1,0:T(8,128)(2,1)S(1)}, u32[]{:S(2)}, u32[]{:S(2)}) collective-permute-start(bf16[128,2048]{1,0:T(8,128)(2,1)S(1)} %get-tuple-element.14), channel_id=1, source_target_pairs={{0,16},{1,17},{2,18},{3,19},{4,20},{5,21},{6,22},{7,23},{8,12},{9,... | collective-permute-start | bytes 1572872 | tf_op jit(solution)/shard_map/ppermute | solution.py:567
  82.7 6.4 %collective-permute-start.2 = (bf16[64,2048]{1,0:T(8,128)(2,1)S(1)}, bf16[64,2048]{1,0:T(8,128)(2,1)S(1)}, u32[]{:S(2)}, u32[]{:S(2)}) collective-permute-start(bf16[64,2048]{1,0:T(8,128)(2,1)S(1)} %get-tuple-element.16), channel_id=1, source_target_pairs={{0,4},{1,5},{2,6},{3,7},{4,0},{5,1},{6,2},{7,3},{8,24},{9,25},{10,... | collective-permute-start | bytes 786440 | tf_op jit(solution)/shard_map/ppermute | solution.py:567
  106.7 12.4 %collective-permute-start.10 = (bf16[128,256]{1,0:T(8,128)(2,1)S(1)}, bf16[128,256]{1,0:T(8,128)(2,1)S(1)}, u32[]{:S(2)}, u32[]{:S(2)}) collective-permute-start(bf16[128,256]{1,0:T(8,128)(2,1)S(1)} %shard_map.97.own_ref), channel_id=1, source_target_pairs={{0,4},{1,5},{2,6},{3,7},{4,0},{5,1},{6,2},{7,3},{8,12},{9,13},{10,... | collective-permute-start | bytes 196616 | tf_op jit(solution)/shard_map/ppermute | solution.py:567
